TPU v7x, 512 devices: a whole 4x4x16 slice. The times are simulated.
512 devices in a mesh: ctx: 64 (over z, x_hi, core), head: 8 (over x_lo, y).
Axes of the slice: x: 4 (x_hi: 2, x_lo: 2; x = x_hi * 2 + x_lo), y: 4, z: 16, core: 2. Of those that a mesh axis runs over, the one named last changes fastest.
Arguments:
- queries: bfloat16 [16384, 4096], P('ctx', 'head'), may hold values from -6 to 6
- key_rows: bfloat16 [16384, 1024], P('ctx', 'head'), may hold values from -6 to 6
- value_rows: bfloat16 [16384, 1024], P('ctx', 'head'), may hold values from -6 to 6
- attn_out: bfloat16 [16384, 4096], P('ctx', 'head'), may hold values from -6 to 6
- out_grad: bfloat16 [16384, 4096], P('ctx', 'head'), may hold values from -6 to 6
- log_sums: float32 [32, 16384], P('head', 'ctx'), may hold values from 4.5 to 6
- block_picks: int32 [128, 32, 3], P('ctx', 'head'), may hold values from 0 to 3, all different within a row
- query_weight: bfloat16 [4096, 4096], P('ctx', 'head'), may hold values from -0.21875 to 0.21875
- key_weight: bfloat16 [4096, 1024], P('ctx', 'head'), may hold values from -0.21875 to 0.21875
- value_weight: bfloat16 [4096, 1024], P('ctx', 'head'), may hold values from -0.21875 to 0.21875
Outputs:
- input_grad: bfloat16 [16384, 4096], P('ctx', 'head')
Inputs may be any that keep to these rules, and one draw needn't show every extreme that they name: `block_picks`: in each row (query block, query head) the 3 entries differ; entry m selects the block m + 1 blocks before the query's block, and selections before the sequence's start select nothing.
All inputs are finite; a program needn't handle non-finite values.
Results may differ from a plain program's by a relative error of at most 0.013.
Values may be sent and summed in bfloat16 or wider, within the bound.
No kernel may reach another device: no remote copies, remote signals or barrier semaphores. Data moves between devices by JAX's collectives and lax.ppermute only.
A program may use at most 64 MiB of HBM per device.

v0:
```python
import functools
import math

import jax
import jax.numpy as jnp
from jax import lax
from jax.experimental import pallas as pl
from jax.experimental.pallas import tpu as pltpu
from jax.sharding import Mesh
from jax.sharding import PartitionSpec as P


BLK = 128
HD = 128
GROUP = 4
BF = jnp.bfloat16
F32 = jnp.float32
Z = ("zh", "zl")
CTX = ("zh", "zl", "xh", "core")
HEAD = ("xl", "y")
NT = (((1,), (1,)), ((), ()))
NN = (((1,), (0,)), ((), ()))
TN = (((0,), (0,)), ((), ()))


def dot(a, b, dims):
    return lax.dot_general(a, b, dims, preferred_element_type=F32)


def passed_along(x, axis, by):
    n = lax.axis_size(axis)
    pairs = [(i, i + by) for i in range(n) if 0 <= i + by < n]
    return lax.ppermute(x, axis, pairs)


def shifted(x, axis, by):
    n = lax.axis_size(axis)
    return lax.ppermute(x, axis, [(i, (i + by) % n) for i in range(n)])


def attention_kernel(
    picks_ref, q_ref, do_ref, o_ref, lse_ref, kv0_ref, kv1_ref, kv2_ref,
    aq_ref, own_ref, ret1_ref, ret2_ref,
):
    scaling = 1.0 / math.sqrt(HD)
    first = lax.axis_index(CTX) * 2
    tables = (kv2_ref, kv2_ref, kv1_ref, kv1_ref, kv0_ref, kv0_ref)
    sums = (ret2_ref, ret2_ref, ret1_ref, ret1_ref, own_ref, own_ref)
    key_at = lax.broadcasted_iota(jnp.int32, (BLK, BLK), 0)
    query_at = lax.broadcasted_iota(jnp.int32, (BLK, BLK), 1)
    causal = key_at <= query_at
    dk = [None] * 6
    dv = [None] * 6
    for b in range(2):
        rows = slice(BLK * b, BLK * b + BLK)
        cols = [slice(HD * h, HD * h + HD) for h in range(GROUP)]
        q = jnp.concatenate([q_ref[rows, c] for c in cols], axis=0)
        do = jnp.concatenate([do_ref[rows, c] for c in cols], axis=0)
        lse = []
        delta = []
        for h in range(GROUP):
            prod = do_ref[rows, cols[h]].astype(F32) * o_ref[rows, cols[h]].astype(F32)
            delta.append(jnp.sum(prod.T, axis=0, keepdims=True))
            lse.append(lse_ref[h : h + 1, rows])
        dq = None
        for s in range(5):
            c = b + s
            half = slice(BLK * (c % 2), BLK * (c % 2) + BLK)
            k = tables[c][half, :HD]
            v = tables[c][half, HD:]
            scores = dot(k, q, NT)
            prob_grad = dot(v, do, NT)
            p_parts = []
            g_parts = []
            for h in range(GROUP):
                at = slice(BLK * h, BLK * h + BLK)
                p = jnp.exp(scores[:, at] * scaling - lse[h])
                if s == 4:
                    p = jnp.where(causal, p, 0.0)
                else:
                    m = 3 - s
                    used = picks_ref[0, b, h] == m
                    for t in range(1, 3):
                        used = used | (picks_ref[t, b, h] == m)
                    used = used & (first + b - 1 - m >= 0)
                    p = jnp.where(used, p, 0.0)
                p_parts.append(p.astype(BF))
                g_parts.append((p * (prob_grad[:, at] - delta[h])).astype(BF))
            p_half = jnp.concatenate(p_parts, axis=1)
            g_half = jnp.concatenate(g_parts, axis=1)
            part = dot(g_half, k, TN)
            dq = part if dq is None else dq + part
            k_part = dot(g_half, q, NN)
            v_part = dot(p_half, do, NN)
            dk[c] = k_part if dk[c] is None else dk[c] + k_part
            dv[c] = v_part if dv[c] is None else dv[c] + v_part
        for h in range(GROUP):
            aq_ref[rows, cols[h]] = (dq[BLK * h : BLK * h + BLK] * scaling).astype(BF)
    for c in range(6):
        half = slice(BLK * (c % 2), BLK * (c % 2) + BLK)
        sums[c][half, :HD] = (dk[c] * scaling).astype(sums[c].dtype)
        sums[c][half, HD:] = dv[c].astype(sums[c].dtype)


def attention(picks, q, do, o, lse, kv0, kv1, kv2):
    tokens = q.shape[0]
    vm = pl.BlockSpec(memory_space=pltpu.VMEM)
    sm = pl.BlockSpec(memory_space=pltpu.SMEM)
    return pl.pallas_call(
        attention_kernel,
        out_shape=(
            pltpu.VMEM(q.shape, BF),
            pltpu.VMEM((tokens, 2 * HD), F32),
            pltpu.VMEM((tokens, 2 * HD), BF),
            pltpu.VMEM((tokens, 2 * HD), BF),
        ),
        in_specs=[sm] + [vm] * 7,
        out_specs=(vm,) * 4,
        name="attention",
    )(
        picks.transpose(2, 0, 1), q, do, o, lse, placed_in(kv0, pltpu.VMEM),
        placed_in(kv1, pltpu.VMEM), placed_in(kv2, pltpu.VMEM),
    )


def project_kernel(side, q_ref, kv_ref, own_hbm, other_ref, *rest):
    out_hbm, w_ref, out_ref, w_sem, out_sem = rest[-5:]
    zl = lax.axis_index("zl")
    xh = lax.axis_index("xh")
    rows_of = xh if side == 0 else 1 - xh
    loads = [
        pltpu.make_async_copy(own_hbm.at[:, zh], w_ref.at[:, zh], w_sem.at[zh]) for zh in range(4)
    ]
    for load in loads:
        load.start()
    stores = []
    for head in range(8):
        zh = head // 2
        if head % 2 == 0:
            loads[zh].wait()
        wide = []
        for e in range(2):
            k = lax.rem(2 * (head % 2) + e + 4 - zl, 4)
            wide += [w_ref[k, zh], other_ref[k, zh]]
        w = jnp.concatenate(wide, axis=0)
        part = dot(q_ref[...], w[:, : GROUP * HD], NT) + dot(kv_ref[...], w[:, GROUP * HD :], NT)
        out_ref[head] = part.astype(BF)
        target = 4 * (head % 4) + 2 * (head // 4) + rows_of
        stores.append(
            pltpu.make_async_copy(out_ref.at[head], out_hbm.at[target], out_sem.at[head])
        )
        stores[-1].start()
    for store in stores:
        store.wait()


def placed_in(x, space):
    return pltpu.with_memory_space_constraint(x, space)


def project(side, aq, akv, wc, wo, parts=None):
    hbm = pl.BlockSpec(memory_space=pltpu.HBM)
    vm = pl.BlockSpec(memory_space=pltpu.VMEM)
    rows, _ = wc.shape[2:]
    extra = () if parts is None else (parts,)
    return pl.pallas_call(
        functools.partial(project_kernel, side),
        out_shape=jax.ShapeDtypeStruct((16, 256, 4 * rows), BF),
        in_specs=[vm, vm, hbm, vm] + [hbm] * len(extra),
        out_specs=hbm,
        scratch_shapes=[
            pltpu.VMEM(wc.shape, BF),
            pltpu.VMEM((8, 256, 4 * rows), BF),
            pltpu.SemaphoreType.DMA((4,)),
            pltpu.SemaphoreType.DMA((8,)),
        ],
        input_output_aliases={4: 0} if extra else {},
    )(placed_in(aq, pltpu.VMEM), placed_in(akv, pltpu.VMEM), wc, placed_in(wo, pltpu.VMEM), *extra)


def total_kernel(in_ref, out_ref):
    swapped = lax.axis_index("core") == 1
    for xh in range(2):
        total = in_ref[xh].astype(F32)
        for h in range(1, 8):
            total = total + in_ref[2 * h + xh].astype(F32)
        for e in range(2):
            at = 256 * e + 128 * xh
            tile = total[:, 128 * e : 128 * e + 128]
            tile = jnp.where(swapped, pltpu.roll(tile, 64, 1), tile)
            out_ref[:, at : at + 128] = tile.astype(BF)


def totalled(parts):
    vm = pl.BlockSpec(memory_space=pltpu.VMEM)
    return pl.pallas_call(
        total_kernel,
        out_shape=jax.ShapeDtypeStruct((parts.shape[1], 512), BF),
        in_specs=[vm],
        out_specs=vm,
        name="total",
    )(placed_in(parts, pltpu.VMEM))


def prepare_kernel(k_ref, v_ref, qw_ref, kw_ref, vw_ref, kv_ref, w_ref):
    kv_ref[:, :HD] = k_ref[...]
    kv_ref[:, HD:] = v_ref[...]
    w_ref[:, : GROUP * HD] = qw_ref[...]
    w_ref[:, GROUP * HD : GROUP * HD + HD] = kw_ref[...]
    w_ref[:, GROUP * HD + HD :] = vw_ref[...]


def prepared(keys, values, qw, kw, vw):
    vm = pl.BlockSpec(memory_space=pltpu.VMEM)
    return pl.pallas_call(
        prepare_kernel,
        out_shape=(
            pltpu.VMEM((keys.shape[0], 2 * HD), BF),
            pltpu.VMEM((qw.shape[0], qw.shape[1] + 2 * HD), BF),
        ),
        in_specs=[vm] * 5,
        out_specs=(vm, vm),
        name="prepare",
    )(keys, values, qw, kw, vw)


def per_device(
    queries, key_rows, value_rows, attn_out, out_grad, log_sums, block_picks,
    query_weight, key_weight, value_weight,
):
    kv0, weight = prepared(key_rows, value_rows, query_weight, key_weight, value_weight)
    w0 = lax.all_gather(weight, "zh")
    kv0, w0 = lax.optimization_barrier((kv0, w0))
    kv1 = passed_along(kv0, CTX, 1)
    kv2 = passed_along(kv0, CTX, 2)
    w1 = shifted(w0, Z, -1)
    w3 = shifted(w0, Z, 1)
    w2 = lax.ppermute(w0, Z, [((z + 2 if z % 2 == 0 else z - 2) % 16, z) for z in range(16)])
    aq, own, ret1, ret2 = attention(
        block_picks, queries, out_grad, attn_out, log_sums, kv0, kv1, kv2
    )
    back1 = passed_along(ret1, CTX, -1)
    back2 = passed_along(ret2, CTX, -2)
    aq_far = shifted(aq, "xh", 1)
    wc = jnp.stack([w0, w1, w2, w3])
    wo = shifted(wc, "core", 1)
    akv = (own + back1.astype(F32) + back2.astype(F32)).astype(BF)
    akv_far = shifted(akv, "xh", 1)
    parts = project(0, aq, akv, wc, wo)
    parts = project(1, aq_far, akv_far, wc, wo, parts)
    parts = lax.all_to_all(parts, ("y", "xl", "xh"), 0, 0)
    return totalled(parts)


def solution(mesh):
    wide = Mesh(
        mesh.devices.reshape(4, 4, 2, 2, 2, 4), ("zh", "zl", "xh", "core", "xl", "y")
    )
    both = P(CTX, HEAD)
    placed = (both,) * 5 + (P(HEAD, CTX), P(CTX, HEAD, None)) + (both,) * 3
    return jax.shard_map(per_device, mesh=wide, in_specs=placed, out_specs=both, check_vma=False)
```

profile of v0, /device:TPU:64, one launch (start us, length us, event | category | flops | bytes accessed | tf_op | source)
XLA Modules:
  0.0 131.5 jit_solution(8607482492462896606)
XLA Ops:
  0.0 1.0 prepare.1
  1.0 28.3 %all-gather = bf16[256,768]{1,0:T(8,128)(2,1)S(1)} all-gather(bf16[64,768]{1,0:T(8,128)(2,1)S(1)} %get-tuple-element.14), channel_id=2, replica_groups=mesh['zh'=4,'zl'=4,'xh'=2,'core'=2,'xl'=2,'y'=4] {'zh'}, dimensions={0}, use_global_device_ids=true | all-gather | bytes 491520 | tf_op jit(solution)/shard_map/all_gather | solution.py:232
  29.3 3.1 %collective-permute-start.8 = (bf16[4,64,768]{2,1,0:T(8,128)(2,1)S(1)}, bf16[4,64,768]{2,1,0:T(8,128)(2,1)S(1)}, u32[]{:S(2)}, u32[]{:S(2)}) collective-permute-start(bf16[4,64,768]{2,1,0:T(8,128)(2,1)S(1)} %bitcast.6), channel_id=1, source_target_pairs={{0,32},{32,64},{64,96},{96,128},{128,160},{160,192},{192,224},{224... | collective-permute-start | bytes 1179656 | tf_op jit(solution)/shard_map/ppermute | solution.py:38
  32.4 3.2 %collective-permute-start.7 = (bf16[4,64,768]{2,1,0:T(8,128)(2,1)S(1)}, bf16[4,64,768]{2,1,0:T(8,128)(2,1)S(1)}, u32[]{:S(2)}, u32[]{:S(2)}) collective-permute-start(bf16[4,64,768]{2,1,0:T(8,128)(2,1)S(1)} %bitcast.7), channel_id=1, source_target_pairs={{64,0},{480,32},{128,64},{32,96},{192,128},{96,160},{256,192},{160... | collective-permute-start | bytes 1179656 | tf_op jit(solution)/shard_map/ppermute | solution.py:238
  35.6 3.1 %collective-permute-start.6 = (bf16[4,64,768]{2,1,0:T(8,128)(2,1)S(1)}, bf16[4,64,768]{2,1,0:T(8,128)(2,1)S(1)}, u32[]{:S(2)}, u32[]{:S(2)}) collective-permute-start(bf16[4,64,768]{2,1,0:T(8,128)(2,1)S(1)} %bitcast.8), channel_id=1, source_target_pairs={{0,480},{32,0},{64,32},{96,64},{128,96},{160,128},{192,160},{224,1... | collective-permute-start | bytes 1179656 | tf_op jit(solution)/shard_map/ppermute | solution.py:38
  38.7 7.6 %collective-permute-done.8 = bf16[4,64,768]{2,1,0:T(8,128)(2,1)S(1)} collective-permute-done((bf16[4,64,768]{2,1,0:T(8,128)(2,1)S(1)}, bf16[4,64,768]{2,1,0:T(8,128)(2,1)S(1)}, u32[]{:S(2)}, u32[]{:S(2)}) %collective-permute-start.8) | collective-permute-done | bytes 393248 | tf_op jit(solution)/shard_map/ppermute | solution.py:38
  46.3 2.0 %collective-permute-done.7 = bf16[4,64,768]{2,1,0:T(8,128)(2,1)S(1)} collective-permute-done((bf16[4,64,768]{2,1,0:T(8,128)(2,1)S(1)}, bf16[4,64,768]{2,1,0:T(8,128)(2,1)S(1)}, u32[]{:S(2)}, u32[]{:S(2)}) %collective-permute-start.7) | collective-permute-done | bytes 393248 | tf_op jit(solution)/shard_map/ppermute | solution.py:238
  48.3 4.1 %collective-permute-done.6 = bf16[4,64,768]{2,1,0:T(8,128)(2,1)S(1)} collective-permute-done((bf16[4,64,768]{2,1,0:T(8,128)(2,1)S(1)}, bf16[4,64,768]{2,1,0:T(8,128)(2,1)S(1)}, u32[]{:S(2)}, u32[]{:S(2)}) %collective-permute-start.6) | collective-permute-done | bytes 393248 | tf_op jit(solution)/shard_map/ppermute | solution.py:38
  52.4 1.4 %pad_maximum_fusion.own_hbm = bf16[4,4,64,768]{3,2,1,0:T(8,128)(2,1)} fusion(bf16[1,4,64,768]{3,2,1,0:T(8,128)(2,1)S(1)} %bitcast.10, bf16[1,4,64,768]{3,2,1,0:T(8,128)(2,1)S(1)} %bitcast.11, bf16[1,4,64,768]{3,2,1,0:T(8,128)(2,1)S(1)} %bitcast.12, bf16[1,4,64,768]{3,2,1,0:T(8,128)(2,1)S(1)} %bitcast.9), kind=kLoop, calls=%fused_computation | loop fusion | flops 2359296 | bytes 3145728 | tf_op jit(solution)/shard_map/stack | solution.py:245
  53.7 1.9 %collective-permute-start.9 = (bf16[4,4,64,768]{3,2,1,0:T(8,128)(2,1)}, bf16[4,4,64,768]{3,2,1,0:T(8,128)(2,1)S(1)}, u32[]{:S(2)}, u32[]{:S(2)}) collective-permute-start(bf16[4,4,64,768]{3,2,1,0:T(8,128)(2,1)} %pad_maximum_fusion.own_hbm), channel_id=1, source_target_pairs={{0,8},{8,0},{1,9},{9,1},{2,10},{10,2},{3,11},{11,3},{4,12},{12,4},... | collective-permute-start | bytes 4718600 | tf_op jit(solution)/shard_map/ppermute | solution.py:38
  55.6 4.9 %collective-permute-start.1 = (bf16[256,256]{1,0:T(8,128)(2,1)S(1)}, bf16[256,256]{1,0:T(8,128)(2,1)S(1)}, u32[]{:S(2)}, u32[]{:S(2)}) collective-permute-start(bf16[256,256]{1,0:T(8,128)(2,1)S(1)} %get-tuple-element.15.kv0_ref), channel_id=1, source_target_pairs={{0,16},{8,24},{16,32},{24,40},{32,48},{40,56},{48,64},{56,72},{64,... | collective-permute-start | bytes 393224 | tf_op jit(solution)/shard_map/ppermute | solution.py:33
  60.6 2.1 %collective-permute-start = (bf16[256,256]{1,0:T(8,128)(2,1)S(1)}, bf16[256,256]{1,0:T(8,128)(2,1)S(1)}, u32[]{:S(2)}, u32[]{:S(2)}) collective-permute-start(bf16[256,256]{1,0:T(8,128)(2,1)S(1)} %get-tuple-element.15.kv0_ref), channel_id=1, source_target_pairs={{0,8},{8,16},{16,24},{24,32},{32,40},{40,48},{48,56},{56,64},{64,7... | collective-permute-start | bytes 393224 | tf_op jit(solution)/shard_map/ppermute | solution.py:33
  62.7 3.1 %collective-permute-done.1.kv2_ref = bf16[256,256]{1,0:T(8,128)(2,1)S(1)} collective-permute-done((bf16[256,256]{1,0:T(8,128)(2,1)S(1)}, bf16[256,256]{1,0:T(8,128)(2,1)S(1)}, u32[]{:S(2)}, u32[]{:S(2)}) %collective-permute-start.1) | collective-permute-done | bytes 131104 | tf_op jit(solution)/shard_map/ppermute | solution.py:33
  65.8 3.4 %collective-permute-done.kv1_ref = bf16[256,256]{1,0:T(8,128)(2,1)S(1)} collective-permute-done((bf16[256,256]{1,0:T(8,128)(2,1)S(1)}, bf16[256,256]{1,0:T(8,128)(2,1)S(1)}, u32[]{:S(2)}, u32[]{:S(2)}) %collective-permute-start) | collective-permute-done | bytes 131104 | tf_op jit(solution)/shard_map/ppermute | solution.py:33
  69.3 4.3 %attention.1 = (bf16[256,512]{1,0:T(8,128)(2,1)S(1)}, f32[256,256]{1,0:T(8,128)S(1)}, bf16[256,256]{1,0:T(8,128)(2,1)S(1)}, bf16[256,256]{1,0:T(8,128)(2,1)S(1)}) custom-call(s32[3,2,4]{2,1,0:T(2,128)} %bitcast.13, bf16[256,512]{1,0:T(8,128)(2,1)} %q_ref.1, bf16[256,512]{1,0:T(8,128)(2,1)} %do_ref.1, bf16[256,512]{1,0:T(8,128)(2,1)} %o_ref.1, ...), custom_call_target="tpu_custom_call" | custom-call | tf_op jit(solution)/shard_map/attention/pallas_call | solution.py:109
  73.6 1.9 %collective-permute-start.3 = (bf16[256,256]{1,0:T(8,128)(2,1)S(1)}, bf16[256,256]{1,0:T(8,128)(2,1)S(1)}, u32[]{:S(2)}, u32[]{:S(2)}) collective-permute-start(bf16[256,256]{1,0:T(8,128)(2,1)S(1)} %get-tuple-element.18), channel_id=1, source_target_pairs={{8,0},{16,8},{24,16},{32,24},{40,32},{48,40},{56,48},{64,56},{72,6... | collective-permute-start | bytes 393224 | tf_op jit(solution)/shard_map/ppermute | solution.py:33
  75.5 2.4 %collective-permute-start.4 = (bf16[256,256]{1,0:T(8,128)(2,1)S(1)}, bf16[256,256]{1,0:T(8,128)(2,1)S(1)}, u32[]{:S(2)}, u32[]{:S(2)}) collective-permute-start(bf16[256,256]{1,0:T(8,128)(2,1)S(1)} %get-tuple-element.19), channel_id=1, source_target_pairs={{16,0},{24,8},{32,16},{40,24},{48,32},{56,40},{64,48},{72,56},{80,... | collective-permute-start | bytes 393224 | tf_op jit(solution)/shard_map/ppermute | solution.py:33
  77.9 4.9 %collective-permute-start.2 = (bf16[256,512]{1,0:T(8,128)(2,1)S(1)}, bf16[256,512]{1,0:T(8,128)(2,1)S(1)}, u32[]{:S(2)}, u32[]{:S(2)}) collective-permute-start(bf16[256,512]{1,0:T(8,128)(2,1)S(1)} %get-tuple-element.16.q_ref), channel_id=1, source_target_pairs={{0,16},{16,0},{1,17},{17,1},{2,18},{18,2},{3,19},{19,3},{4,20},{20... | collective-permute-start | bytes 786440 | tf_op jit(solution)/shard_map/ppermute | solution.py:38
  82.9 0.0 collective-permute-done.3
  82.9 2.4 %collective-permute-done.4 = bf16[256,256]{1,0:T(8,128)(2,1)S(1)} collective-permute-done((bf16[256,256]{1,0:T(8,128)(2,1)S(1)}, bf16[256,256]{1,0:T(8,128)(2,1)S(1)}, u32[]{:S(2)}, u32[]{:S(2)}) %collective-permute-start.4) | collective-permute-done | bytes 131104 | tf_op jit(solution)/shard_map/ppermute | solution.py:33
  85.3 0.1 add_convert_fusion.kv_ref
  85.3 2.4 %collective-permute-start.5 = (bf16[256,256]{1,0:T(8,128)(2,1)S(1)}, bf16[256,256]{1,0:T(8,128)(2,1)S(1)}, u32[]{:S(2)}, u32[]{:S(2)}) collective-permute-start(bf16[256,256]{1,0:T(8,128)(2,1)S(1)} %add_convert_fusion.kv_ref), channel_id=1, source_target_pairs={{0,16},{16,0},{1,17},{17,1},{2,18},{18,2},{3,19},{19,3},{4,20},{20... | collective-permute-start | bytes 393224 | tf_op jit(solution)/shard_map/ppermute | solution.py:38
  87.8 0.0 collective-permute-done.9.other_ref
  87.8 3.4 %shard_map.100.rest_0_ = bf16[16,256,256]{2,1,0:T(8,128)(2,1)} custom-call(bf16[256,512]{1,0:T(8,128)(2,1)S(1)} %get-tuple-element.16.q_ref, bf16[256,256]{1,0:T(8,128)(2,1)S(1)} %add_convert_fusion.kv_ref, bf16[4,4,64,768]{3,2,1,0:T(8,128)(2,1)} %pad_maximum_fusion.own_hbm, bf16[4,4,64,768]{3,2,1,0:T(8,128)(2,1)S(1)} %collective-permute-done.9.other_ref), custom_call_target="tpu_custom_call" | custom-call | tf_op jit(solution)/shard_map/pallas_call | solution.py:166
  91.2 2.5 %collective-permute-done.5.kv_ref = bf16[256,256]{1,0:T(8,128)(2,1)S(1)} collective-permute-done((bf16[256,256]{1,0:T(8,128)(2,1)S(1)}, bf16[256,256]{1,0:T(8,128)(2,1)S(1)}, u32[]{:S(2)}, u32[]{:S(2)}) %collective-permute-start.5) | collective-permute-done | bytes 131104 | tf_op jit(solution)/shard_map/ppermute | solution.py:38
  93.7 0.0 collective-permute-done.2.q_ref
  93.7 3.4 %shard_map.101 = bf16[16,256,256]{2,1,0:T(8,128)(2,1)} custom-call(bf16[256,512]{1,0:T(8,128)(2,1)S(1)} %collective-permute-done.2.q_ref, bf16[256,256]{1,0:T(8,128)(2,1)S(1)} %collective-permute-done.5.kv_ref, bf16[4,4,64,768]{3,2,1,0:T(8,128)(2,1)} %pad_maximum_fusion.own_hbm, ...), custom_call_target="tpu_custom_call", output_to_operand_aliasing={{}: (4, {})} | custom-call | tf_op jit(solution)/shard_map/pallas_call | solution.py:166
  97.2 33.3 %all_to_all.5.in_ref = bf16[16,256,256]{2,1,0:T(8,128)(2,1)S(1)} all-to-all(bf16[16,256,256]{2,1,0:T(8,128)(2,1)} %shard_map.101), channel_id=1, replica_groups=mesh['zh'=4,'zl'=4,'xh'=2,'core'=2,'xl'=2,'y'=4] {'y','xl','xh'}, dimensions={0} | all-to-all | bytes 4194304 | tf_op jit(solution)/shard_map/all_to_all | solution.py:251
  130.4 1.0 total.1
Async XLA Ops:
  29.3 17.0 %collective-permute-start.8 = (bf16[4,64,768]{2,1,0:T(8,128)(2,1)S(1)}, bf16[4,64,768]{2,1,0:T(8,128)(2,1)S(1)}, u32[]{:S(2)}, u32[]{:S(2)}) collective-permute-start(bf16[4,64,768]{2,1,0:T(8,128)(2,1)S(1)} %bitcast.6), channel_id=1, source_target_pairs={{0,32},{32,64},{64,96},{96,128},{128,160},{160,192},{192,224},{224... | collective-permute-start | bytes 1179656 | tf_op jit(solution)/shard_map/ppermute | solution.py:38
  32.4 15.9 %collective-permute-start.7 = (bf16[4,64,768]{2,1,0:T(8,128)(2,1)S(1)}, bf16[4,64,768]{2,1,0:T(8,128)(2,1)S(1)}, u32[]{:S(2)}, u32[]{:S(2)}) collective-permute-start(bf16[4,64,768]{2,1,0:T(8,128)(2,1)S(1)} %bitcast.7), channel_id=1, source_target_pairs={{64,0},{480,32},{128,64},{32,96},{192,128},{96,160},{256,192},{160... | collective-permute-start | bytes 1179656 | tf_op jit(solution)/shard_map/ppermute | solution.py:238
  35.6 16.8 %collective-permute-start.6 = (bf16[4,64,768]{2,1,0:T(8,128)(2,1)S(1)}, bf16[4,64,768]{2,1,0:T(8,128)(2,1)S(1)}, u32[]{:S(2)}, u32[]{:S(2)}) collective-permute-start(bf16[4,64,768]{2,1,0:T(8,128)(2,1)S(1)} %bitcast.8), channel_id=1, source_target_pairs={{0,480},{32,0},{64,32},{96,64},{128,96},{160,128},{192,160},{224,1... | collective-permute-start | bytes 1179656 | tf_op jit(solution)/shard_map/ppermute | solution.py:38
  53.7 34.1 %collective-permute-start.9 = (bf16[4,4,64,768]{3,2,1,0:T(8,128)(2,1)}, bf16[4,4,64,768]{3,2,1,0:T(8,128)(2,1)S(1)}, u32[]{:S(2)}, u32[]{:S(2)}) collective-permute-start(bf16[4,4,64,768]{3,2,1,0:T(8,128)(2,1)} %pad_maximum_fusion.own_hbm), channel_id=1, source_target_pairs={{0,8},{8,0},{1,9},{9,1},{2,10},{10,2},{3,11},{11,3},{4,12},{12,4},... | collective-permute-start | bytes 4718600 | tf_op jit(solution)/shard_map/ppermute | solution.py:38
  55.6 10.2 %collective-permute-start.1 = (bf16[256,256]{1,0:T(8,128)(2,1)S(1)}, bf16[256,256]{1,0:T(8,128)(2,1)S(1)}, u32[]{:S(2)}, u32[]{:S(2)}) collective-permute-start(bf16[256,256]{1,0:T(8,128)(2,1)S(1)} %get-tuple-element.15.kv0_ref), channel_id=1, source_target_pairs={{0,16},{8,24},{16,32},{24,40},{32,48},{40,56},{48,64},{56,72},{64,... | collective-permute-start | bytes 393224 | tf_op jit(solution)/shard_map/ppermute | solution.py:33
  60.6 8.7 %collective-permute-start = (bf16[256,256]{1,0:T(8,128)(2,1)S(1)}, bf16[256,256]{1,0:T(8,128)(2,1)S(1)}, u32[]{:S(2)}, u32[]{:S(2)}) collective-permute-start(bf16[256,256]{1,0:T(8,128)(2,1)S(1)} %get-tuple-element.15.kv0_ref), channel_id=1, source_target_pairs={{0,8},{8,16},{16,24},{24,32},{32,40},{40,48},{48,56},{56,64},{64,7... | collective-permute-start | bytes 393224 | tf_op jit(solution)/shard_map/ppermute | solution.py:33
  73.6 9.3 %collective-permute-start.3 = (bf16[256,256]{1,0:T(8,128)(2,1)S(1)}, bf16[256,256]{1,0:T(8,128)(2,1)S(1)}, u32[]{:S(2)}, u32[]{:S(2)}) collective-permute-start(bf16[256,256]{1,0:T(8,128)(2,1)S(1)} %get-tuple-element.18), channel_id=1, source_target_pairs={{8,0},{16,8},{24,16},{32,24},{40,32},{48,40},{56,48},{64,56},{72,6... | collective-permute-start | bytes 393224 | tf_op jit(solution)/shard_map/ppermute | solution.py:33
  75.5 9.8 %collective-permute-start.4 = (bf16[256,256]{1,0:T(8,128)(2,1)S(1)}, bf16[256,256]{1,0:T(8,128)(2,1)S(1)}, u32[]{:S(2)}, u32[]{:S(2)}) collective-permute-start(bf16[256,256]{1,0:T(8,128)(2,1)S(1)} %get-tuple-element.19), channel_id=1, source_target_pairs={{16,0},{24,8},{32,16},{40,24},{48,32},{56,40},{64,48},{72,56},{80,... | collective-permute-start | bytes 393224 | tf_op jit(solution)/shard_map/ppermute | solution.py:33
  77.9 15.8 %collective-permute-start.2 = (bf16[256,512]{1,0:T(8,128)(2,1)S(1)}, bf16[256,512]{1,0:T(8,128)(2,1)S(1)}, u32[]{:S(2)}, u32[]{:S(2)}) collective-permute-start(bf16[256,512]{1,0:T(8,128)(2,1)S(1)} %get-tuple-element.16.q_ref), channel_id=1, source_target_pairs={{0,16},{16,0},{1,17},{17,1},{2,18},{18,2},{3,19},{19,3},{4,20},{20... | collective-permute-start | bytes 786440 | tf_op jit(solution)/shard_map/ppermute | solution.py:38
  85.3 8.4 %collective-permute-start.5 = (bf16[256,256]{1,0:T(8,128)(2,1)S(1)}, bf16[256,256]{1,0:T(8,128)(2,1)S(1)}, u32[]{:S(2)}, u32[]{:S(2)}) collective-permute-start(bf16[256,256]{1,0:T(8,128)(2,1)S(1)} %add_convert_fusion.kv_ref), channel_id=1, source_target_pairs={{0,16},{16,0},{1,17},{17,1},{2,18},{18,2},{3,19},{19,3},{4,20},{20... | collective-permute-start | bytes 393224 | tf_op jit(solution)/shard_map/ppermute | solution.py:38
where the time goes:
time: 132 us; the launch traced here: 131 us
  blocking collectives  61.6 us (47%)
  starting transfers between devices  30.1 us (23%)
  waiting for transfers between devices  25.1 us (19%)
  Pallas kernels  13.2 us (10%)
  other arithmetic  1.41 us (1%)
    all_to_all x1, blocking collectives, per_device(): parts = lax.all_to_all(parts, ('y', 'xl', 'xh'), 0, 0)  33.3 us
    all_gather x1, blocking collectives, per_device(): w0 = lax.all_gather(weight, 'zh')  28.3 us
    ppermute x5, starting transfers between devices, shifted(): return lax.ppermute(x, axis, [(i, (i + by) % n) for i in range(n)])  15.5 us
    ppermute x5, waiting for transfers between devices, shifted(): return lax.ppermute(x, axis, [(i, (i + by) % n) for i in range(n)])  14.1 us
    ppermute x4, starting transfers between devices, passed_along(): return lax.ppermute(x, axis, pairs)  11.4 us
    ppermute x4, waiting for transfers between devices, passed_along(): return lax.ppermute(x, axis, pairs)  8.95 us
    pallas_call x2, Pallas kernels, project(): pl.pallas_call(functools.partial(project_kernel, side), out_shape=jax.Sha...  6.88 us
    pallas_call x1, Pallas kernels, attention(): pl.pallas_call(attention_kernel, out_shape=(pltpu.VMEM(q.shape, BF), pltp...  4.32 us
  transfers between devices with their start and end apart: 10, of which 7 were waited for; matrix products, arithmetic and copies ran while one was open for 0% of the time, Pallas kernels for 6%

commit v1 on v0

--- a/solution.py
+++ b/solution.py
@@ -127,7 +127,7 @@
     out_hbm, w_ref, out_ref, w_sem, out_sem = rest[-5:]
     zl = lax.axis_index("zl")
     xh = lax.axis_index("xh")
-    rows_of = xh if side == 0 else 1 - xh
+    first = 8 * (xh if side == 0 else 1 - xh)
     loads = [
         pltpu.make_async_copy(own_hbm.at[:, zh], w_ref.at[:, zh], w_sem.at[zh]) for zh in range(4)
     ]
@@ -145,9 +145,8 @@
         w = jnp.concatenate(wide, axis=0)
         part = dot(q_ref[...], w[:, : GROUP * HD], NT) + dot(kv_ref[...], w[:, GROUP * HD :], NT)
         out_ref[head] = part.astype(BF)
-        target = 4 * (head % 4) + 2 * (head // 4) + rows_of
         stores.append(
-            pltpu.make_async_copy(out_ref.at[head], out_hbm.at[target], out_sem.at[head])
+            pltpu.make_async_copy(out_ref.at[head], out_hbm.at[first + head], out_sem.at[head])
         )
         stores[-1].start()
     for store in stores:
@@ -181,9 +180,9 @@
 def total_kernel(in_ref, out_ref):
     swapped = lax.axis_index("core") == 1
     for xh in range(2):
-        total = in_ref[xh].astype(F32)
+        total = in_ref[8 * xh].astype(F32)
         for h in range(1, 8):
-            total = total + in_ref[2 * h + xh].astype(F32)
+            total = total + in_ref[8 * xh + h].astype(F32)
         for e in range(2):
             at = 256 * e + 128 * xh
             tile = total[:, 128 * e : 128 * e + 128]
@@ -229,10 +228,9 @@
     query_weight, key_weight, value_weight,
 ):
     kv0, weight = prepared(key_rows, value_rows, query_weight, key_weight, value_weight)
-    w0 = lax.all_gather(weight, "zh")
-    kv0, w0 = lax.optimization_barrier((kv0, w0))
     kv1 = passed_along(kv0, CTX, 1)
     kv2 = passed_along(kv0, CTX, 2)
+    w0 = lax.all_gather(weight, "zh")
     w1 = shifted(w0, Z, -1)
     w3 = shifted(w0, Z, 1)
     w2 = lax.ppermute(w0, Z, [((z + 2 if z % 2 == 0 else z - 2) % 16, z) for z in range(16)])
@@ -248,8 +246,8 @@
     akv_far = shifted(akv, "xh", 1)
     parts = project(0, aq, akv, wc, wo)
     parts = project(1, aq_far, akv_far, wc, wo, parts)
-    parts = lax.all_to_all(parts, ("y", "xl", "xh"), 0, 0)
-    return totalled(parts)
+    parts = lax.all_to_all(parts.transpose(1, 0, 2), ("xh", "xl", "y"), 1, 1)
+    return totalled(parts.transpose(1, 0, 2))
 
 
 def solution(mesh):

time: 132 us -> 130 us (0.985)
  the two profiles are of different devices: /device:TPU:64 before, /device:TPU:32 now
where the time goes in v1:
time: 130 us; the launch traced here: 129 us
  blocking collectives  63.2 us (49%)
  starting transfers between devices  30.2 us (23%)
  waiting for transfers between devices  21.1 us (16%)
  Pallas kernels  13.2 us (10%)
  other arithmetic  1.4 us (1%)
    all_to_all x1, blocking collectives, per_device(): parts = lax.all_to_all(parts.transpose(1, 0, 2), ('xh', 'xl', 'y'), 1, 1)  33.9 us
    all_gather x1, blocking collectives, per_device(): w0 = lax.all_gather(weight, 'zh')  29.2 us
    ppermute x5, starting transfers between devices, shifted(): return lax.ppermute(x, axis, [(i, (i + by) % n) for i in range(n)])  14.9 us
    ppermute x4, starting transfers between devices, passed_along(): return lax.ppermute(x, axis, pairs)  11.8 us
    ppermute x4, waiting for transfers between devices, passed_along(): return lax.ppermute(x, axis, pairs)  8.78 us
    ppermute x5, waiting for transfers between devices, shifted(): return lax.ppermute(x, axis, [(i, (i + by) % n) for i in range(n)])  7.25 us
    pallas_call x2, Pallas kernels, project(): pl.pallas_call(functools.partial(project_kernel, side), out_shape=jax.Sha...  6.9 us
    ppermute x1, waiting for transfers between devices, per_device(): lax.ppermute(w0, Z, [((z + 2 if z % 2 == 0 else z - 2) % 16, z) for z in...  5.05 us
  transfers between devices with their start and end apart: 10, of which 7 were waited for; matrix products, arithmetic and copies ran while one was open for 0% of the time, Pallas kernels for 6%

profile of v1, /device:TPU:32, one launch (start us, length us, event | category | flops | bytes accessed | tf_op | source)
XLA Modules:
  0.0 129.2 jit_solution(15377298368017997735)
XLA Ops:
  0.0 1.0 prepare.1
  1.0 29.2 %all-gather = bf16[256,768]{1,0:T(8,128)(2,1)S(1)} all-gather(bf16[64,768]{1,0:T(8,128)(2,1)S(1)} %get-tuple-element.16), channel_id=2, replica_groups=mesh['zh'=4,'zl'=4,'xh'=2,'core'=2,'xl'=2,'y'=4] {'zh'}, dimensions={0}, use_global_device_ids=true | all-gather | bytes 491520 | tf_op jit(solution)/shard_map/all_gather | solution.py:233
  30.2 3.5 %collective-permute-start.7 = (bf16[4,64,768]{2,1,0:T(8,128)(2,1)S(1)}, bf16[4,64,768]{2,1,0:T(8,128)(2,1)S(1)}, u32[]{:S(2)}, u32[]{:S(2)}) collective-permute-start(bf16[4,64,768]{2,1,0:T(8,128)(2,1)S(1)} %bitcast.10), channel_id=1, source_target_pairs={{64,0},{480,32},{128,64},{32,96},{192,128},{96,160},{256,192},{160... | collective-permute-start | bytes 1179656 | tf_op jit(solution)/shard_map/ppermute | solution.py:236
  33.7 3.1 %collective-permute-start.6 = (bf16[4,64,768]{2,1,0:T(8,128)(2,1)S(1)}, bf16[4,64,768]{2,1,0:T(8,128)(2,1)S(1)}, u32[]{:S(2)}, u32[]{:S(2)}) collective-permute-start(bf16[4,64,768]{2,1,0:T(8,128)(2,1)S(1)} %bitcast.11), channel_id=1, source_target_pairs={{0,480},{32,0},{64,32},{96,64},{128,96},{160,128},{192,160},{224,1... | collective-permute-start | bytes 1179656 | tf_op jit(solution)/shard_map/ppermute | solution.py:38
  36.9 2.7 %collective-permute-start.8 = (bf16[4,64,768]{2,1,0:T(8,128)(2,1)S(1)}, bf16[4,64,768]{2,1,0:T(8,128)(2,1)S(1)}, u32[]{:S(2)}, u32[]{:S(2)}) collective-permute-start(bf16[4,64,768]{2,1,0:T(8,128)(2,1)S(1)} %bitcast.12), channel_id=1, source_target_pairs={{0,32},{32,64},{64,96},{96,128},{128,160},{160,192},{192,224},{224... | collective-permute-start | bytes 1179656 | tf_op jit(solution)/shard_map/ppermute | solution.py:38
  39.6 5.0 %collective-permute-done.7 = bf16[4,64,768]{2,1,0:T(8,128)(2,1)S(1)} collective-permute-done((bf16[4,64,768]{2,1,0:T(8,128)(2,1)S(1)}, bf16[4,64,768]{2,1,0:T(8,128)(2,1)S(1)}, u32[]{:S(2)}, u32[]{:S(2)}) %collective-permute-start.7) | collective-permute-done | bytes 393248 | tf_op jit(solution)/shard_map/ppermute | solution.py:236
  44.7 4.0 %collective-permute-done.6 = bf16[4,64,768]{2,1,0:T(8,128)(2,1)S(1)} collective-permute-done((bf16[4,64,768]{2,1,0:T(8,128)(2,1)S(1)}, bf16[4,64,768]{2,1,0:T(8,128)(2,1)S(1)}, u32[]{:S(2)}, u32[]{:S(2)}) %collective-permute-start.6) | collective-permute-done | bytes 393248 | tf_op jit(solution)/shard_map/ppermute | solution.py:38
  48.7 0.9 collective-permute-done.8
  49.6 1.4 %pad_maximum_fusion.own_hbm = bf16[4,4,64,768]{3,2,1,0:T(8,128)(2,1)} fusion(bf16[1,4,64,768]{3,2,1,0:T(8,128)(2,1)S(1)} %bitcast.16, bf16[1,4,64,768]{3,2,1,0:T(8,128)(2,1)S(1)} %bitcast.14, bf16[1,4,64,768]{3,2,1,0:T(8,128)(2,1)S(1)} %bitcast.15, bf16[1,4,64,768]{3,2,1,0:T(8,128)(2,1)S(1)} %bitcast.13), kind=kLoop, calls=%fused_computation | loop fusion | flops 2359296 | bytes 3145728 | tf_op jit(solution)/shard_map/stack | solution.py:243
  51.0 1.9 %collective-permute-start.9 = (bf16[4,4,64,768]{3,2,1,0:T(8,128)(2,1)}, bf16[4,4,64,768]{3,2,1,0:T(8,128)(2,1)S(1)}, u32[]{:S(2)}, u32[]{:S(2)}) collective-permute-start(bf16[4,4,64,768]{3,2,1,0:T(8,128)(2,1)} %pad_maximum_fusion.own_hbm), channel_id=1, source_target_pairs={{0,8},{8,0},{1,9},{9,1},{2,10},{10,2},{3,11},{11,3},{4,12},{12,4},... | collective-permute-start | bytes 4718600 | tf_op jit(solution)/shard_map/ppermute | solution.py:38
  52.9 4.9 %collective-permute-start.1 = (bf16[256,256]{1,0:T(8,128)(2,1)S(1)}, bf16[256,256]{1,0:T(8,128)(2,1)S(1)}, u32[]{:S(2)}, u32[]{:S(2)}) collective-permute-start(bf16[256,256]{1,0:T(8,128)(2,1)S(1)} %get-tuple-element.11.kv0_ref), channel_id=1, source_target_pairs={{0,16},{8,24},{16,32},{24,40},{32,48},{40,56},{48,64},{56,72},{64,... | collective-permute-start | bytes 393224 | tf_op jit(solution)/shard_map/ppermute | solution.py:33
  57.8 2.1 %collective-permute-start = (bf16[256,256]{1,0:T(8,128)(2,1)S(1)}, bf16[256,256]{1,0:T(8,128)(2,1)S(1)}, u32[]{:S(2)}, u32[]{:S(2)}) collective-permute-start(bf16[256,256]{1,0:T(8,128)(2,1)S(1)} %get-tuple-element.11.kv0_ref), channel_id=1, source_target_pairs={{0,8},{8,16},{16,24},{24,32},{32,40},{40,48},{48,56},{56,64},{64,7... | collective-permute-start | bytes 393224 | tf_op jit(solution)/shard_map/ppermute | solution.py:33
  60.0 3.1 %collective-permute-done.1.kv2_ref = bf16[256,256]{1,0:T(8,128)(2,1)S(1)} collective-permute-done((bf16[256,256]{1,0:T(8,128)(2,1)S(1)}, bf16[256,256]{1,0:T(8,128)(2,1)S(1)}, u32[]{:S(2)}, u32[]{:S(2)}) %collective-permute-start.1) | collective-permute-done | bytes 131104 | tf_op jit(solution)/shard_map/ppermute | solution.py:33
  63.1 3.4 %collective-permute-done.kv1_ref = bf16[256,256]{1,0:T(8,128)(2,1)S(1)} collective-permute-done((bf16[256,256]{1,0:T(8,128)(2,1)S(1)}, bf16[256,256]{1,0:T(8,128)(2,1)S(1)}, u32[]{:S(2)}, u32[]{:S(2)}) %collective-permute-start) | collective-permute-done | bytes 131104 | tf_op jit(solution)/shard_map/ppermute | solution.py:33
  66.5 4.3 %attention.1 = (bf16[256,512]{1,0:T(8,128)(2,1)S(1)}, f32[256,256]{1,0:T(8,128)S(1)}, bf16[256,256]{1,0:T(8,128)(2,1)S(1)}, bf16[256,256]{1,0:T(8,128)(2,1)S(1)}) custom-call(s32[3,2,4]{2,1,0:T(2,128)} %bitcast.17, bf16[256,512]{1,0:T(8,128)(2,1)} %q_ref.1, bf16[256,512]{1,0:T(8,128)(2,1)} %do_ref.1, bf16[256,512]{1,0:T(8,128)(2,1)} %o_ref.1, ...), custom_call_target="tpu_custom_call" | custom-call | tf_op jit(solution)/shard_map/attention/pallas_call | solution.py:109
  70.9 1.9 %collective-permute-start.3 = (bf16[256,256]{1,0:T(8,128)(2,1)S(1)}, bf16[256,256]{1,0:T(8,128)(2,1)S(1)}, u32[]{:S(2)}, u32[]{:S(2)}) collective-permute-start(bf16[256,256]{1,0:T(8,128)(2,1)S(1)} %get-tuple-element.14), channel_id=1, source_target_pairs={{8,0},{16,8},{24,16},{32,24},{40,32},{48,40},{56,48},{64,56},{72,6... | collective-permute-start | bytes 393224 | tf_op jit(solution)/shard_map/ppermute | solution.py:33
  72.8 2.8 %collective-permute-start.4 = (bf16[256,256]{1,0:T(8,128)(2,1)S(1)}, bf16[256,256]{1,0:T(8,128)(2,1)S(1)}, u32[]{:S(2)}, u32[]{:S(2)}) collective-permute-start(bf16[256,256]{1,0:T(8,128)(2,1)S(1)} %get-tuple-element.15), channel_id=1, source_target_pairs={{16,0},{24,8},{32,16},{40,24},{48,32},{56,40},{64,48},{72,56},{80,... | collective-permute-start | bytes 393224 | tf_op jit(solution)/shard_map/ppermute | solution.py:33
  75.6 4.6 %collective-permute-start.2 = (bf16[256,512]{1,0:T(8,128)(2,1)S(1)}, bf16[256,512]{1,0:T(8,128)(2,1)S(1)}, u32[]{:S(2)}, u32[]{:S(2)}) collective-permute-start(bf16[256,512]{1,0:T(8,128)(2,1)S(1)} %get-tuple-element.12.q_ref), channel_id=1, source_target_pairs={{0,16},{16,0},{1,17},{17,1},{2,18},{18,2},{3,19},{19,3},{4,20},{20... | collective-permute-start | bytes 786440 | tf_op jit(solution)/shard_map/ppermute | solution.py:38
  80.1 0.0 collective-permute-done.3
  80.2 2.2 %collective-permute-done.4 = bf16[256,256]{1,0:T(8,128)(2,1)S(1)} collective-permute-done((bf16[256,256]{1,0:T(8,128)(2,1)S(1)}, bf16[256,256]{1,0:T(8,128)(2,1)S(1)}, u32[]{:S(2)}, u32[]{:S(2)}) %collective-permute-start.4) | collective-permute-done | bytes 131104 | tf_op jit(solution)/shard_map/ppermute | solution.py:33
  82.4 2.6 %collective-permute-start.5 = (bf16[256,256]{1,0:T(8,128)(2,1)S(1)}, bf16[256,256]{1,0:T(8,128)(2,1)S(1)}, u32[]{:S(2)}, u32[]{:S(2)}) collective-permute-start(bf16[256,256]{1,0:T(8,128)(2,1)S(1)} %add_convert_fusion.kv_ref), channel_id=1, source_target_pairs={{0,16},{16,0},{1,17},{17,1},{2,18},{18,2},{3,19},{19,3},{4,20},{20... | collective-permute-start | bytes 393224 | tf_op jit(solution)/shard_map/ppermute | solution.py:38
  85.1 0.0 collective-permute-done.9.other_ref
  85.1 3.4 %shard_map.100.rest_0_ = bf16[16,256,256]{2,1,0:T(8,128)(2,1)} custom-call(bf16[256,512]{1,0:T(8,128)(2,1)S(1)} %get-tuple-element.12.q_ref, bf16[256,256]{1,0:T(8,128)(2,1)S(1)} %add_convert_fusion.kv_ref, bf16[4,4,64,768]{3,2,1,0:T(8,128)(2,1)} %pad_maximum_fusion.own_hbm, bf16[4,4,64,768]{3,2,1,0:T(8,128)(2,1)S(1)} %collective-permute-done.9.other_ref), custom_call_target="tpu_custom_call" | custom-call | tf_op jit(solution)/shard_map/pallas_call | solution.py:165
  88.5 2.3 %collective-permute-done.5.kv_ref = bf16[256,256]{1,0:T(8,128)(2,1)S(1)} collective-permute-done((bf16[256,256]{1,0:T(8,128)(2,1)S(1)}, bf16[256,256]{1,0:T(8,128)(2,1)S(1)}, u32[]{:S(2)}, u32[]{:S(2)}) %collective-permute-start.5) | collective-permute-done | bytes 131104 | tf_op jit(solution)/shard_map/ppermute | solution.py:38
  90.8 0.0 collective-permute-done.2.q_ref
  90.8 3.5 %shard_map.101 = bf16[16,256,256]{2,1,0:T(8,128)(2,1)} custom-call(bf16[256,512]{1,0:T(8,128)(2,1)S(1)} %collective-permute-done.2.q_ref, bf16[256,256]{1,0:T(8,128)(2,1)S(1)} %collective-permute-done.5.kv_ref, bf16[4,4,64,768]{3,2,1,0:T(8,128)(2,1)} %pad_maximum_fusion.own_hbm, ...), custom_call_target="tpu_custom_call", output_to_operand_aliasing={{}: (4, {})} | custom-call | tf_op jit(solution)/shard_map/pallas_call | solution.py:165
  94.3 33.9 %all_to_all.5 = bf16[256,16,256]{2,0,1:T(8,128)(2,1)S(1)} all-to-all(bf16[256,16,256]{2,0,1:T(8,128)(2,1)} %bitcast.9), channel_id=1, replica_groups=mesh['zh'=4,'zl'=4,'xh'=2,'core'=2,'xl'=2,'y'=4] {'xh','xl','y'}, dimensions={1} | all-to-all | bytes 4194304 | tf_op jit(solution)/shard_map/all_to_all | solution.py:249
  128.2 1.0 total.1
  (1 shorter events, 0.0 us)
Async XLA Ops:
  30.2 14.5 %collective-permute-start.7 = (bf16[4,64,768]{2,1,0:T(8,128)(2,1)S(1)}, bf16[4,64,768]{2,1,0:T(8,128)(2,1)S(1)}, u32[]{:S(2)}, u32[]{:S(2)}) collective-permute-start(bf16[4,64,768]{2,1,0:T(8,128)(2,1)S(1)} %bitcast.10), channel_id=1, source_target_pairs={{64,0},{480,32},{128,64},{32,96},{192,128},{96,160},{256,192},{160... | collective-permute-start | bytes 1179656 | tf_op jit(solution)/shard_map/ppermute | solution.py:236
  33.7 14.9 %collective-permute-start.6 = (bf16[4,64,768]{2,1,0:T(8,128)(2,1)S(1)}, bf16[4,64,768]{2,1,0:T(8,128)(2,1)S(1)}, u32[]{:S(2)}, u32[]{:S(2)}) collective-permute-start(bf16[4,64,768]{2,1,0:T(8,128)(2,1)S(1)} %bitcast.11), channel_id=1, source_target_pairs={{0,480},{32,0},{64,32},{96,64},{128,96},{160,128},{192,160},{224,1... | collective-permute-start | bytes 1179656 | tf_op jit(solution)/shard_map/ppermute | solution.py:38
  36.9 12.8 %collective-permute-start.8 = (bf16[4,64,768]{2,1,0:T(8,128)(2,1)S(1)}, bf16[4,64,768]{2,1,0:T(8,128)(2,1)S(1)}, u32[]{:S(2)}, u32[]{:S(2)}) collective-permute-start(bf16[4,64,768]{2,1,0:T(8,128)(2,1)S(1)} %bitcast.12), channel_id=1, source_target_pairs={{0,32},{32,64},{64,96},{96,128},{128,160},{160,192},{192,224},{224... | collective-permute-start | bytes 1179656 | tf_op jit(solution)/shard_map/ppermute | solution.py:38
  51.0 34.1 %collective-permute-start.9 = (bf16[4,4,64,768]{3,2,1,0:T(8,128)(2,1)}, bf16[4,4,64,768]{3,2,1,0:T(8,128)(2,1)S(1)}, u32[]{:S(2)}, u32[]{:S(2)}) collective-permute-start(bf16[4,4,64,768]{3,2,1,0:T(8,128)(2,1)} %pad_maximum_fusion.own_hbm), channel_id=1, source_target_pairs={{0,8},{8,0},{1,9},{9,1},{2,10},{10,2},{3,11},{11,3},{4,12},{12,4},... | collective-permute-start | bytes 4718600 | tf_op jit(solution)/shard_map/ppermute | solution.py:38
  52.9 10.2 %collective-permute-start.1 = (bf16[256,256]{1,0:T(8,128)(2,1)S(1)}, bf16[256,256]{1,0:T(8,128)(2,1)S(1)}, u32[]{:S(2)}, u32[]{:S(2)}) collective-permute-start(bf16[256,256]{1,0:T(8,128)(2,1)S(1)} %get-tuple-element.11.kv0_ref), channel_id=1, source_target_pairs={{0,16},{8,24},{16,32},{24,40},{32,48},{40,56},{48,64},{56,72},{64,... | collective-permute-start | bytes 393224 | tf_op jit(solution)/shard_map/ppermute | solution.py:33
  57.8 8.7 %collective-permute-start = (bf16[256,256]{1,0:T(8,128)(2,1)S(1)}, bf16[256,256]{1,0:T(8,128)(2,1)S(1)}, u32[]{:S(2)}, u32[]{:S(2)}) collective-permute-start(bf16[256,256]{1,0:T(8,128)(2,1)S(1)} %get-tuple-element.11.kv0_ref), channel_id=1, source_target_pairs={{0,8},{8,16},{16,24},{24,32},{32,40},{40,48},{48,56},{56,64},{64,7... | collective-permute-start | bytes 393224 | tf_op jit(solution)/shard_map/ppermute | solution.py:33
  70.9 9.3 %collective-permute-start.3 = (bf16[256,256]{1,0:T(8,128)(2,1)S(1)}, bf16[256,256]{1,0:T(8,128)(2,1)S(1)}, u32[]{:S(2)}, u32[]{:S(2)}) collective-permute-start(bf16[256,256]{1,0:T(8,128)(2,1)S(1)} %get-tuple-element.14), channel_id=1, source_target_pairs={{8,0},{16,8},{24,16},{32,24},{40,32},{48,40},{56,48},{64,56},{72,6... | collective-permute-start | bytes 393224 | tf_op jit(solution)/shard_map/ppermute | solution.py:33
  72.8 9.6 %collective-permute-start.4 = (bf16[256,256]{1,0:T(8,128)(2,1)S(1)}, bf16[256,256]{1,0:T(8,128)(2,1)S(1)}, u32[]{:S(2)}, u32[]{:S(2)}) collective-permute-start(bf16[256,256]{1,0:T(8,128)(2,1)S(1)} %get-tuple-element.15), channel_id=1, source_target_pairs={{16,0},{24,8},{32,16},{40,24},{48,32},{56,40},{64,48},{72,56},{80,... | collective-permute-start | bytes 393224 | tf_op jit(solution)/shard_map/ppermute | solution.py:33
  75.6 15.2 %collective-permute-start.2 = (bf16[256,512]{1,0:T(8,128)(2,1)S(1)}, bf16[256,512]{1,0:T(8,128)(2,1)S(1)}, u32[]{:S(2)}, u32[]{:S(2)}) collective-permute-start(bf16[256,512]{1,0:T(8,128)(2,1)S(1)} %get-tuple-element.12.q_ref), channel_id=1, source_target_pairs={{0,16},{16,0},{1,17},{17,1},{2,18},{18,2},{3,19},{19,3},{4,20},{20... | collective-permute-start | bytes 786440 | tf_op jit(solution)/shard_map/ppermute | solution.py:38
  82.4 8.4 %collective-permute-start.5 = (bf16[256,256]{1,0:T(8,128)(2,1)S(1)}, bf16[256,256]{1,0:T(8,128)(2,1)S(1)}, u32[]{:S(2)}, u32[]{:S(2)}) collective-permute-start(bf16[256,256]{1,0:T(8,128)(2,1)S(1)} %add_convert_fusion.kv_ref), channel_id=1, source_target_pairs={{0,16},{16,0},{1,17},{17,1},{2,18},{18,2},{3,19},{19,3},{4,20},{20... | collective-permute-start | bytes 393224 | tf_op jit(solution)/shard_map/ppermute | solution.py:38

commit v2 on v1

--- a/solution.py
+++ b/solution.py
@@ -39,12 +39,21 @@
 
 
 def attention_kernel(
-    picks_ref, q_ref, do_ref, o_ref, lse_ref, kv0_ref, kv1_ref, kv2_ref,
+    picks_ref, q_ref, do_ref, o_ref, lse_ref, here_ref, prev_ref,
     aq_ref, own_ref, ret1_ref, ret2_ref,
 ):
     scaling = 1.0 / math.sqrt(HD)
     first = lax.axis_index(CTX) * 2
-    tables = (kv2_ref, kv2_ref, kv1_ref, kv1_ref, kv0_ref, kv0_ref)
+    core = lax.axis_index("core")
+
+    def table(c, cols):
+        half = slice(BLK * (c % 2), BLK * (c % 2) + BLK)
+        if c < 2:
+            return prev_ref[core, half, cols]
+        if c < 4:
+            return jnp.where(core == 0, prev_ref[1, half, cols], here_ref[0, half, cols])
+        return here_ref[core, half, cols]
+
     sums = (ret2_ref, ret2_ref, ret1_ref, ret1_ref, own_ref, own_ref)
     key_at = lax.broadcasted_iota(jnp.int32, (BLK, BLK), 0)
     query_at = lax.broadcasted_iota(jnp.int32, (BLK, BLK), 1)
@@ -65,9 +74,8 @@
         dq = None
         for s in range(5):
             c = b + s
-            half = slice(BLK * (c % 2), BLK * (c % 2) + BLK)
-            k = tables[c][half, :HD]
-            v = tables[c][half, HD:]
+            k = table(c, slice(0, HD))
+            v = table(c, slice(HD, 2 * HD))
             scores = dot(k, q, NT)
             prob_grad = dot(v, do, NT)
             p_parts = []
@@ -102,7 +110,7 @@
         sums[c][half, HD:] = dv[c].astype(sums[c].dtype)
 
 
-def attention(picks, q, do, o, lse, kv0, kv1, kv2):
+def attention(picks, q, do, o, lse, here, prev):
     tokens = q.shape[0]
     vm = pl.BlockSpec(memory_space=pltpu.VMEM)
     sm = pl.BlockSpec(memory_space=pltpu.SMEM)
@@ -114,12 +122,12 @@
             pltpu.VMEM((tokens, 2 * HD), BF),
             pltpu.VMEM((tokens, 2 * HD), BF),
         ),
-        in_specs=[sm] + [vm] * 7,
+        in_specs=[sm] + [vm] * 6,
         out_specs=(vm,) * 4,
         name="attention",
     )(
-        picks.transpose(2, 0, 1), q, do, o, lse, placed_in(kv0, pltpu.VMEM),
-        placed_in(kv1, pltpu.VMEM), placed_in(kv2, pltpu.VMEM),
+        picks.transpose(2, 0, 1), q, do, o, lse,
+        placed_in(here, pltpu.VMEM), placed_in(prev, pltpu.VMEM),
     )
 
 
@@ -228,15 +236,13 @@
     query_weight, key_weight, value_weight,
 ):
     kv0, weight = prepared(key_rows, value_rows, query_weight, key_weight, value_weight)
-    kv1 = passed_along(kv0, CTX, 1)
-    kv2 = passed_along(kv0, CTX, 2)
+    here = lax.all_gather(kv0, "core")
+    prev = passed_along(here, CTX, 2)
     w0 = lax.all_gather(weight, "zh")
     w1 = shifted(w0, Z, -1)
     w3 = shifted(w0, Z, 1)
     w2 = lax.ppermute(w0, Z, [((z + 2 if z % 2 == 0 else z - 2) % 16, z) for z in range(16)])
-    aq, own, ret1, ret2 = attention(
-        block_picks, queries, out_grad, attn_out, log_sums, kv0, kv1, kv2
-    )
+    aq, own, ret1, ret2 = attention(block_picks, queries, out_grad, attn_out, log_sums, here, prev)
     back1 = passed_along(ret1, CTX, -1)
     back2 = passed_along(ret2, CTX, -2)
     aq_far = shifted(aq, "xh", 1)
@@ -246,8 +252,8 @@
     akv_far = shifted(akv, "xh", 1)
     parts = project(0, aq, akv, wc, wo)
     parts = project(1, aq_far, akv_far, wc, wo, parts)
-    parts = lax.all_to_all(parts.transpose(1, 0, 2), ("xh", "xl", "y"), 1, 1)
-    return totalled(parts.transpose(1, 0, 2))
+    parts = lax.all_to_all(parts, ("xh", "xl", "y"), 0, 0)
+    return totalled(parts)
 
 
 def solution(mesh):

time: 130 us -> 133 us (1.023)
  blocking collectives: 63.2 us -> 65.5 us
    all_gather x0 -> x1, blocking collectives: none -> 3.77 us  [per_device(): here = lax.all_gather(kv0, 'core')]
    all_to_all x1, blocking collectives: 33.9 us -> 32.5 us  [per_device(): parts = lax.all_to_all(parts, ('xh', 'xl', 'y'), 0, 0)]
    ppermute x4 -> x3, starting transfers between devices: 11.8 us -> 11.6 us  [passed_along(): return lax.ppermute(x, axis, pairs)]
    ppermute x4 -> x3, waiting for transfers between devices: 8.78 us -> 8.7 us  [passed_along(): return lax.ppermute(x, axis, pairs)]
  transfers between devices with their start and end apart: 10 -> 9, of which waited for: 7 -> 6; matrix products, arithmetic and copies ran while one was open for 0% -> 0% of each run, Pallas kernels for 6% -> 6%
where the time goes in v2:
time: 133 us; the launch traced here: 132 us
  blocking collectives  65.5 us (49%)
  starting transfers between devices  31.4 us (24%)
  waiting for transfers between devices  20.3 us (15%)
  Pallas kernels  13.2 us (10%)
  other arithmetic  1.42 us (1%)
    all_to_all x1, blocking collectives, per_device(): parts = lax.all_to_all(parts, ('xh', 'xl', 'y'), 0, 0)  32.5 us
    all_gather x1, blocking collectives, per_device(): w0 = lax.all_gather(weight, 'zh')  29.2 us
    ppermute x5, starting transfers between devices, shifted(): return lax.ppermute(x, axis, [(i, (i + by) % n) for i in range(n)])  16.2 us
    ppermute x3, starting transfers between devices, passed_along(): return lax.ppermute(x, axis, pairs)  11.6 us
    ppermute x3, waiting for transfers between devices, passed_along(): return lax.ppermute(x, axis, pairs)  8.7 us
    pallas_call x2, Pallas kernels, project(): pl.pallas_call(functools.partial(project_kernel, side), out_shape=jax.Sha...  6.9 us
    ppermute x5, waiting for transfers between devices, shifted(): return lax.ppermute(x, axis, [(i, (i + by) % n) for i in range(n)])  6.6 us
    ppermute x1, waiting for transfers between devices, per_device(): lax.ppermute(w0, Z, [((z + 2 if z % 2 == 0 else z - 2) % 16, z) for z in...  5.05 us
  transfers between devices with their start and end apart: 9, of which 6 were waited for; matrix products, arithmetic and copies ran while one was open for 0% of the time, Pallas kernels for 6%

profile of v2, /device:TPU:32, one launch (start us, length us, event | category | flops | bytes accessed | tf_op | source)
XLA Modules:
  0.0 132.0 jit_solution(3738313395715011398)
XLA Ops:
  0.0 1.0 prepare.1
  1.0 29.2 %all-gather.1 = bf16[256,768]{1,0:T(8,128)(2,1)S(1)} all-gather(bf16[64,768]{1,0:T(8,128)(2,1)S(1)} %get-tuple-element.16), channel_id=3, replica_groups=mesh['zh'=4,'zl'=4,'xh'=2,'core'=2,'xl'=2,'y'=4] {'zh'}, dimensions={0}, use_global_device_ids=true | all-gather | bytes 491520 | tf_op jit(solution)/shard_map/all_gather | solution.py:241
  30.2 3.5 %collective-permute-start.6 = (bf16[4,64,768]{2,1,0:T(8,128)(2,1)S(1)}, bf16[4,64,768]{2,1,0:T(8,128)(2,1)S(1)}, u32[]{:S(2)}, u32[]{:S(2)}) collective-permute-start(bf16[4,64,768]{2,1,0:T(8,128)(2,1)S(1)} %bitcast.9), channel_id=1, source_target_pairs={{64,0},{480,32},{128,64},{32,96},{192,128},{96,160},{256,192},{160... | collective-permute-start | bytes 1179656 | tf_op jit(solution)/shard_map/ppermute | solution.py:244
  33.7 3.1 %collective-permute-start.5 = (bf16[4,64,768]{2,1,0:T(8,128)(2,1)S(1)}, bf16[4,64,768]{2,1,0:T(8,128)(2,1)S(1)}, u32[]{:S(2)}, u32[]{:S(2)}) collective-permute-start(bf16[4,64,768]{2,1,0:T(8,128)(2,1)S(1)} %bitcast.10), channel_id=1, source_target_pairs={{0,480},{32,0},{64,32},{96,64},{128,96},{160,128},{192,160},{224,1... | collective-permute-start | bytes 1179656 | tf_op jit(solution)/shard_map/ppermute | solution.py:38
  36.9 2.7 %collective-permute-start.7 = (bf16[4,64,768]{2,1,0:T(8,128)(2,1)S(1)}, bf16[4,64,768]{2,1,0:T(8,128)(2,1)S(1)}, u32[]{:S(2)}, u32[]{:S(2)}) collective-permute-start(bf16[4,64,768]{2,1,0:T(8,128)(2,1)S(1)} %bitcast.11), channel_id=1, source_target_pairs={{0,32},{32,64},{64,96},{96,128},{128,160},{160,192},{192,224},{224... | collective-permute-start | bytes 1179656 | tf_op jit(solution)/shard_map/ppermute | solution.py:38
  39.6 5.0 %collective-permute-done.6 = bf16[4,64,768]{2,1,0:T(8,128)(2,1)S(1)} collective-permute-done((bf16[4,64,768]{2,1,0:T(8,128)(2,1)S(1)}, bf16[4,64,768]{2,1,0:T(8,128)(2,1)S(1)}, u32[]{:S(2)}, u32[]{:S(2)}) %collective-permute-start.6) | collective-permute-done | bytes 393248 | tf_op jit(solution)/shard_map/ppermute | solution.py:244
  44.7 4.0 %collective-permute-done.5 = bf16[4,64,768]{2,1,0:T(8,128)(2,1)S(1)} collective-permute-done((bf16[4,64,768]{2,1,0:T(8,128)(2,1)S(1)}, bf16[4,64,768]{2,1,0:T(8,128)(2,1)S(1)}, u32[]{:S(2)}, u32[]{:S(2)}) %collective-permute-start.5) | collective-permute-done | bytes 393248 | tf_op jit(solution)/shard_map/ppermute | solution.py:38
  48.7 0.9 collective-permute-done.7
  49.6 1.4 %pad_maximum_fusion.own_hbm = bf16[4,4,64,768]{3,2,1,0:T(8,128)(2,1)} fusion(bf16[1,4,64,768]{3,2,1,0:T(8,128)(2,1)S(1)} %bitcast.15, bf16[1,4,64,768]{3,2,1,0:T(8,128)(2,1)S(1)} %bitcast.13, bf16[1,4,64,768]{3,2,1,0:T(8,128)(2,1)S(1)} %bitcast.14, bf16[1,4,64,768]{3,2,1,0:T(8,128)(2,1)S(1)} %bitcast.12), kind=kLoop, calls=%fused_computation | loop fusion | flops 2359296 | bytes 3145728 | tf_op jit(solution)/shard_map/stack | solution.py:249
  51.0 1.9 %collective-permute-start.8 = (bf16[4,4,64,768]{3,2,1,0:T(8,128)(2,1)}, bf16[4,4,64,768]{3,2,1,0:T(8,128)(2,1)S(1)}, u32[]{:S(2)}, u32[]{:S(2)}) collective-permute-start(bf16[4,4,64,768]{3,2,1,0:T(8,128)(2,1)} %pad_maximum_fusion.own_hbm), channel_id=1, source_target_pairs={{0,8},{8,0},{1,9},{9,1},{2,10},{10,2},{3,11},{11,3},{4,12},{12,4},... | collective-permute-start | bytes 4718600 | tf_op jit(solution)/shard_map/ppermute | solution.py:38
  52.9 3.8 %all-gather = bf16[512,256]{1,0:T(8,128)(2,1)S(1)} all-gather(bf16[256,256]{1,0:T(8,128)(2,1)S(1)} %get-tuple-element.11), channel_id=2, replica_groups=mesh['zh'=4,'zl'=4,'xh'=2,'core'=2,'xl'=2,'y'=4] {'core'}, dimensions={0}, use_global_device_ids=true | all-gather | bytes 393216 | tf_op jit(solution)/shard_map/all_gather | solution.py:239
  56.7 4.9 %collective-permute-start = (bf16[2,256,256]{2,1,0:T(8,128)(2,1)S(1)}, bf16[2,256,256]{2,1,0:T(8,128)(2,1)S(1)}, u32[]{:S(2)}, u32[]{:S(2)}) collective-permute-start(bf16[2,256,256]{2,1,0:T(8,128)(2,1)S(1)} %bitcast.7), channel_id=1, source_target_pairs={{0,16},{8,24},{16,32},{24,40},{32,48},{40,56},{48,64},{56,72},{64,... | collective-permute-start | bytes 786440 | tf_op jit(solution)/shard_map/ppermute | solution.py:33
  61.6 7.7 %collective-permute-done.prev_ref = bf16[2,256,256]{2,1,0:T(8,128)(2,1)S(1)} collective-permute-done((bf16[2,256,256]{2,1,0:T(8,128)(2,1)S(1)}, bf16[2,256,256]{2,1,0:T(8,128)(2,1)S(1)}, u32[]{:S(2)}, u32[]{:S(2)}) %collective-permute-start) | collective-permute-done | bytes 262176 | tf_op jit(solution)/shard_map/ppermute | solution.py:33
  69.3 4.3 %attention.1 = (bf16[256,512]{1,0:T(8,128)(2,1)S(1)}, f32[256,256]{1,0:T(8,128)S(1)}, bf16[256,256]{1,0:T(8,128)(2,1)S(1)}, bf16[256,256]{1,0:T(8,128)(2,1)S(1)}) custom-call(s32[3,2,4]{2,1,0:T(2,128)} %bitcast.16, bf16[256,512]{1,0:T(8,128)(2,1)} %q_ref.1, bf16[256,512]{1,0:T(8,128)(2,1)} %do_ref.1, bf16[256,512]{1,0:T(8,128)(2,1)} %o_ref.1, ...), custom_call_target="tpu_custom_call" | custom-call | tf_op jit(solution)/shard_map/attention/pallas_call | solution.py:117
  73.6 3.7 %collective-permute-start.2 = (bf16[256,256]{1,0:T(8,128)(2,1)S(1)}, bf16[256,256]{1,0:T(8,128)(2,1)S(1)}, u32[]{:S(2)}, u32[]{:S(2)}) collective-permute-start(bf16[256,256]{1,0:T(8,128)(2,1)S(1)} %get-tuple-element.14), channel_id=1, source_target_pairs={{8,0},{16,8},{24,16},{32,24},{40,32},{48,40},{56,48},{64,56},{72,6... | collective-permute-start | bytes 393224 | tf_op jit(solution)/shard_map/ppermute | solution.py:33
  77.3 3.0 %collective-permute-start.3 = (bf16[256,256]{1,0:T(8,128)(2,1)S(1)}, bf16[256,256]{1,0:T(8,128)(2,1)S(1)}, u32[]{:S(2)}, u32[]{:S(2)}) collective-permute-start(bf16[256,256]{1,0:T(8,128)(2,1)S(1)} %get-tuple-element.15), channel_id=1, source_target_pairs={{16,0},{24,8},{32,16},{40,24},{48,32},{56,40},{64,48},{72,56},{80,... | collective-permute-start | bytes 393224 | tf_op jit(solution)/shard_map/ppermute | solution.py:33
  80.4 4.3 %collective-permute-start.1 = (bf16[256,512]{1,0:T(8,128)(2,1)S(1)}, bf16[256,512]{1,0:T(8,128)(2,1)S(1)}, u32[]{:S(2)}, u32[]{:S(2)}) collective-permute-start(bf16[256,512]{1,0:T(8,128)(2,1)S(1)} %get-tuple-element.12.q_ref), channel_id=1, source_target_pairs={{0,16},{16,0},{1,17},{17,1},{2,18},{18,2},{3,19},{19,3},{4,20},{20... | collective-permute-start | bytes 786440 | tf_op jit(solution)/shard_map/ppermute | solution.py:38
  84.7 0.0 collective-permute-done.2
  84.7 1.0 collective-permute-done.3
  85.8 4.2 %collective-permute-start.4 = (bf16[256,256]{1,0:T(8,128)(2,1)S(1)}, bf16[256,256]{1,0:T(8,128)(2,1)S(1)}, u32[]{:S(2)}, u32[]{:S(2)}) collective-permute-start(bf16[256,256]{1,0:T(8,128)(2,1)S(1)} %add_convert_fusion.kv_ref), channel_id=1, source_target_pairs={{0,16},{16,0},{1,17},{17,1},{2,18},{18,2},{3,19},{19,3},{4,20},{20... | collective-permute-start | bytes 393224 | tf_op jit(solution)/shard_map/ppermute | solution.py:38
  89.9 0.0 collective-permute-done.8.other_ref
  89.9 3.4 %shard_map.100.rest_0_ = bf16[16,256,256]{2,1,0:T(8,128)(2,1)} custom-call(bf16[256,512]{1,0:T(8,128)(2,1)S(1)} %get-tuple-element.12.q_ref, bf16[256,256]{1,0:T(8,128)(2,1)S(1)} %add_convert_fusion.kv_ref, bf16[4,4,64,768]{3,2,1,0:T(8,128)(2,1)} %pad_maximum_fusion.own_hbm, bf16[4,4,64,768]{3,2,1,0:T(8,128)(2,1)S(1)} %collective-permute-done.8.other_ref), custom_call_target="tpu_custom_call" | custom-call | tf_op jit(solution)/shard_map/pallas_call | solution.py:173
  93.4 1.6 %collective-permute-done.4.kv_ref = bf16[256,256]{1,0:T(8,128)(2,1)S(1)} collective-permute-done((bf16[256,256]{1,0:T(8,128)(2,1)S(1)}, bf16[256,256]{1,0:T(8,128)(2,1)S(1)}, u32[]{:S(2)}, u32[]{:S(2)}) %collective-permute-start.4) | collective-permute-done | bytes 131104 | tf_op jit(solution)/shard_map/ppermute | solution.py:38
  95.0 0.0 collective-permute-done.1.q_ref
  95.0 3.5 %shard_map.101 = bf16[16,256,256]{2,1,0:T(8,128)(2,1)} custom-call(bf16[256,512]{1,0:T(8,128)(2,1)S(1)} %collective-permute-done.1.q_ref, bf16[256,256]{1,0:T(8,128)(2,1)S(1)} %collective-permute-done.4.kv_ref, bf16[4,4,64,768]{3,2,1,0:T(8,128)(2,1)} %pad_maximum_fusion.own_hbm, ...), custom_call_target="tpu_custom_call", output_to_operand_aliasing={{}: (4, {})} | custom-call | tf_op jit(solution)/shard_map/pallas_call | solution.py:173
  98.5 32.5 %all_to_all.5.in_ref = bf16[16,256,256]{2,1,0:T(8,128)(2,1)S(1)} all-to-all(bf16[16,256,256]{2,1,0:T(8,128)(2,1)} %shard_map.101), channel_id=1, replica_groups=mesh['zh'=4,'zl'=4,'xh'=2,'core'=2,'xl'=2,'y'=4] {'xh','xl','y'}, dimensions={0} | all-to-all | bytes 4194304 | tf_op jit(solution)/shard_map/all_to_all | solution.py:255
  131.0 1.0 total.1
  (1 shorter events, 0.0 us)
Async XLA Ops:
  30.2 14.5 %collective-permute-start.6 = (bf16[4,64,768]{2,1,0:T(8,128)(2,1)S(1)}, bf16[4,64,768]{2,1,0:T(8,128)(2,1)S(1)}, u32[]{:S(2)}, u32[]{:S(2)}) collective-permute-start(bf16[4,64,768]{2,1,0:T(8,128)(2,1)S(1)} %bitcast.9), channel_id=1, source_target_pairs={{64,0},{480,32},{128,64},{32,96},{192,128},{96,160},{256,192},{160... | collective-permute-start | bytes 1179656 | tf_op jit(solution)/shard_map/ppermute | solution.py:244
  33.7 14.9 %collective-permute-start.5 = (bf16[4,64,768]{2,1,0:T(8,128)(2,1)S(1)}, bf16[4,64,768]{2,1,0:T(8,128)(2,1)S(1)}, u32[]{:S(2)}, u32[]{:S(2)}) collective-permute-start(bf16[4,64,768]{2,1,0:T(8,128)(2,1)S(1)} %bitcast.10), channel_id=1, source_target_pairs={{0,480},{32,0},{64,32},{96,64},{128,96},{160,128},{192,160},{224,1... | collective-permute-start | bytes 1179656 | tf_op jit(solution)/shard_map/ppermute | solution.py:38
  36.9 12.8 %collective-permute-start.7 = (bf16[4,64,768]{2,1,0:T(8,128)(2,1)S(1)}, bf16[4,64,768]{2,1,0:T(8,128)(2,1)S(1)}, u32[]{:S(2)}, u32[]{:S(2)}) collective-permute-start(bf16[4,64,768]{2,1,0:T(8,128)(2,1)S(1)} %bitcast.11), channel_id=1, source_target_pairs={{0,32},{32,64},{64,96},{96,128},{128,160},{160,192},{192,224},{224... | collective-permute-start | bytes 1179656 | tf_op jit(solution)/shard_map/ppermute | solution.py:38
  51.0 38.9 %collective-permute-start.8 = (bf16[4,4,64,768]{3,2,1,0:T(8,128)(2,1)}, bf16[4,4,64,768]{3,2,1,0:T(8,128)(2,1)S(1)}, u32[]{:S(2)}, u32[]{:S(2)}) collective-permute-start(bf16[4,4,64,768]{3,2,1,0:T(8,128)(2,1)} %pad_maximum_fusion.own_hbm), channel_id=1, source_target_pairs={{0,8},{8,0},{1,9},{9,1},{2,10},{10,2},{3,11},{11,3},{4,12},{12,4},... | collective-permute-start | bytes 4718600 | tf_op jit(solution)/shard_map/ppermute | solution.py:38
  56.7 12.6 %collective-permute-start = (bf16[2,256,256]{2,1,0:T(8,128)(2,1)S(1)}, bf16[2,256,256]{2,1,0:T(8,128)(2,1)S(1)}, u32[]{:S(2)}, u32[]{:S(2)}) collective-permute-start(bf16[2,256,256]{2,1,0:T(8,128)(2,1)S(1)} %bitcast.7), channel_id=1, source_target_pairs={{0,16},{8,24},{16,32},{24,40},{32,48},{40,56},{48,64},{56,72},{64,... | collective-permute-start | bytes 786440 | tf_op jit(solution)/shard_map/ppermute | solution.py:33
  73.6 11.1 %collective-permute-start.2 = (bf16[256,256]{1,0:T(8,128)(2,1)S(1)}, bf16[256,256]{1,0:T(8,128)(2,1)S(1)}, u32[]{:S(2)}, u32[]{:S(2)}) collective-permute-start(bf16[256,256]{1,0:T(8,128)(2,1)S(1)} %get-tuple-element.14), channel_id=1, source_target_pairs={{8,0},{16,8},{24,16},{32,24},{40,32},{48,40},{56,48},{64,56},{72,6... | collective-permute-start | bytes 393224 | tf_op jit(solution)/shard_map/ppermute | solution.py:33
  77.3 8.4 %collective-permute-start.3 = (bf16[256,256]{1,0:T(8,128)(2,1)S(1)}, bf16[256,256]{1,0:T(8,128)(2,1)S(1)}, u32[]{:S(2)}, u32[]{:S(2)}) collective-permute-start(bf16[256,256]{1,0:T(8,128)(2,1)S(1)} %get-tuple-element.15), channel_id=1, source_target_pairs={{16,0},{24,8},{32,16},{40,24},{48,32},{56,40},{64,48},{72,56},{80,... | collective-permute-start | bytes 393224 | tf_op jit(solution)/shard_map/ppermute | solution.py:33
  80.4 14.6 %collective-permute-start.1 = (bf16[256,512]{1,0:T(8,128)(2,1)S(1)}, bf16[256,512]{1,0:T(8,128)(2,1)S(1)}, u32[]{:S(2)}, u32[]{:S(2)}) collective-permute-start(bf16[256,512]{1,0:T(8,128)(2,1)S(1)} %get-tuple-element.12.q_ref), channel_id=1, source_target_pairs={{0,16},{16,0},{1,17},{17,1},{2,18},{18,2},{3,19},{19,3},{4,20},{20... | collective-permute-start | bytes 786440 | tf_op jit(solution)/shard_map/ppermute | solution.py:38
  85.8 9.3 %collective-permute-start.4 = (bf16[256,256]{1,0:T(8,128)(2,1)S(1)}, bf16[256,256]{1,0:T(8,128)(2,1)S(1)}, u32[]{:S(2)}, u32[]{:S(2)}) collective-permute-start(bf16[256,256]{1,0:T(8,128)(2,1)S(1)} %add_convert_fusion.kv_ref), channel_id=1, source_target_pairs={{0,16},{16,0},{1,17},{17,1},{2,18},{18,2},{3,19},{19,3},{4,20},{20... | collective-permute-start | bytes 393224 | tf_op jit(solution)/shard_map/ppermute | solution.py:38

commit v3 on v1

--- a/solution.py
+++ b/solution.py
@@ -62,7 +62,8 @@
             prod = do_ref[rows, cols[h]].astype(F32) * o_ref[rows, cols[h]].astype(F32)
             delta.append(jnp.sum(prod.T, axis=0, keepdims=True))
             lse.append(lse_ref[h : h + 1, rows])
-        dq = None
+        keys = []
+        g_all = []
         for s in range(5):
             c = b + s
             half = slice(BLK * (c % 2), BLK * (c % 2) + BLK)
@@ -88,12 +89,13 @@
                 g_parts.append((p * (prob_grad[:, at] - delta[h])).astype(BF))
             p_half = jnp.concatenate(p_parts, axis=1)
             g_half = jnp.concatenate(g_parts, axis=1)
-            part = dot(g_half, k, TN)
-            dq = part if dq is None else dq + part
+            keys.append(k)
+            g_all.append(g_half)
             k_part = dot(g_half, q, NN)
             v_part = dot(p_half, do, NN)
             dk[c] = k_part if dk[c] is None else dk[c] + k_part
             dv[c] = v_part if dv[c] is None else dv[c] + v_part
+        dq = dot(jnp.concatenate(g_all, axis=0), jnp.concatenate(keys, axis=0), TN)
         for h in range(GROUP):
             aq_ref[rows, cols[h]] = (dq[BLK * h : BLK * h + BLK] * scaling).astype(BF)
     for c in range(6):
@@ -133,6 +135,7 @@
     ]
     for load in loads:
         load.start()
+    a = jnp.concatenate([q_ref[...], kv_ref[...]], axis=1)
     stores = []
     for head in range(8):
         zh = head // 2
@@ -143,8 +146,7 @@
             k = lax.rem(2 * (head % 2) + e + 4 - zl, 4)
             wide += [w_ref[k, zh], other_ref[k, zh]]
         w = jnp.concatenate(wide, axis=0)
-        part = dot(q_ref[...], w[:, : GROUP * HD], NT) + dot(kv_ref[...], w[:, GROUP * HD :], NT)
-        out_ref[head] = part.astype(BF)
+        out_ref[head] = dot(a, w, NT).astype(BF)
         stores.append(
             pltpu.make_async_copy(out_ref.at[head], out_hbm.at[first + head], out_sem.at[head])
         )
@@ -246,8 +248,8 @@
     akv_far = shifted(akv, "xh", 1)
     parts = project(0, aq, akv, wc, wo)
     parts = project(1, aq_far, akv_far, wc, wo, parts)
-    parts = lax.all_to_all(parts.transpose(1, 0, 2), ("xh", "xl", "y"), 1, 1)
-    return totalled(parts.transpose(1, 0, 2))
+    parts = lax.all_to_all(parts, ("xh", "xl", "y"), 0, 0)
+    return totalled(parts)
 
 
 def solution(mesh):
@@ -256,4 +258,6 @@
     )
     both = P(CTX, HEAD)
     placed = (both,) * 5 + (P(HEAD, CTX), P(CTX, HEAD, None)) + (both,) * 3
-    return jax.shard_map(per_device, mesh=wide, in_specs=placed, out_specs=both, check_vma=False)
+    return jax.shard_map(
+        per_device, mesh=wide, in_specs=placed, out_specs=both, check_vma=False
+    )

time: 130 us -> 129 us (level)
  no operation moved by 1% of the time
where the time goes in v3:
time: 129 us
  blocking collectives  63.2 us (49%)
  starting transfers between devices  30.2 us (23%)
  waiting for transfers between devices  21.1 us (16%)
  Pallas kernels  12.6 us (10%)
  other arithmetic  1.41 us (1%)
    all_to_all x1, blocking collectives, per_device(): parts = lax.all_to_all(parts, ('xh', 'xl', 'y'), 0, 0)  33.9 us
    all_gather x1, blocking collectives, per_device(): w0 = lax.all_gather(weight, 'zh')  29.2 us
    ppermute x5, starting transfers between devices, shifted(): return lax.ppermute(x, axis, [(i, (i + by) % n) for i in range(n)])  14.9 us
    ppermute x4, starting transfers between devices, passed_along(): return lax.ppermute(x, axis, pairs)  11.8 us
    ppermute x4, waiting for transfers between devices, passed_along(): return lax.ppermute(x, axis, pairs)  8.78 us
    ppermute x5, waiting for transfers between devices, shifted(): return lax.ppermute(x, axis, [(i, (i + by) % n) for i in range(n)])  7.25 us
    pallas_call x2, Pallas kernels, project(): pl.pallas_call(functools.partial(project_kernel, side), out_shape=jax.Sha...  6.9 us
    ppermute x1, waiting for transfers between devices, per_device(): lax.ppermute(w0, Z, [((z + 2 if z % 2 == 0 else z - 2) % 16, z) for z in...  5.05 us
  transfers between devices with their start and end apart: 10, of which 7 were waited for; matrix products, arithmetic and copies ran while one was open for 0% of the time, Pallas kernels for 6%

profile of v3, /device:TPU:32, one launch (start us, length us, event | category | flops | bytes accessed | tf_op | source)
XLA Modules:
  0.0 128.6 jit_solution(5594008552606912059)
XLA Ops:
  0.0 1.0 prepare.1
  1.0 29.2 %all-gather = bf16[256,768]{1,0:T(8,128)(2,1)S(1)} all-gather(bf16[64,768]{1,0:T(8,128)(2,1)S(1)} %get-tuple-element.16), channel_id=2, replica_groups=mesh['zh'=4,'zl'=4,'xh'=2,'core'=2,'xl'=2,'y'=4] {'zh'}, dimensions={0}, use_global_device_ids=true | all-gather | bytes 491520 | tf_op jit(solution)/shard_map/all_gather | solution.py:235
  30.2 3.5 %collective-permute-start.7 = (bf16[4,64,768]{2,1,0:T(8,128)(2,1)S(1)}, bf16[4,64,768]{2,1,0:T(8,128)(2,1)S(1)}, u32[]{:S(2)}, u32[]{:S(2)}) collective-permute-start(bf16[4,64,768]{2,1,0:T(8,128)(2,1)S(1)} %bitcast.6), channel_id=1, source_target_pairs={{64,0},{480,32},{128,64},{32,96},{192,128},{96,160},{256,192},{160... | collective-permute-start | bytes 1179656 | tf_op jit(solution)/shard_map/ppermute | solution.py:238
  33.7 3.1 %collective-permute-start.6 = (bf16[4,64,768]{2,1,0:T(8,128)(2,1)S(1)}, bf16[4,64,768]{2,1,0:T(8,128)(2,1)S(1)}, u32[]{:S(2)}, u32[]{:S(2)}) collective-permute-start(bf16[4,64,768]{2,1,0:T(8,128)(2,1)S(1)} %bitcast.7), channel_id=1, source_target_pairs={{0,480},{32,0},{64,32},{96,64},{128,96},{160,128},{192,160},{224,1... | collective-permute-start | bytes 1179656 | tf_op jit(solution)/shard_map/ppermute | solution.py:38
  36.9 2.7 %collective-permute-start.8 = (bf16[4,64,768]{2,1,0:T(8,128)(2,1)S(1)}, bf16[4,64,768]{2,1,0:T(8,128)(2,1)S(1)}, u32[]{:S(2)}, u32[]{:S(2)}) collective-permute-start(bf16[4,64,768]{2,1,0:T(8,128)(2,1)S(1)} %bitcast.8), channel_id=1, source_target_pairs={{0,32},{32,64},{64,96},{96,128},{128,160},{160,192},{192,224},{224... | collective-permute-start | bytes 1179656 | tf_op jit(solution)/shard_map/ppermute | solution.py:38
  39.6 5.0 %collective-permute-done.7 = bf16[4,64,768]{2,1,0:T(8,128)(2,1)S(1)} collective-permute-done((bf16[4,64,768]{2,1,0:T(8,128)(2,1)S(1)}, bf16[4,64,768]{2,1,0:T(8,128)(2,1)S(1)}, u32[]{:S(2)}, u32[]{:S(2)}) %collective-permute-start.7) | collective-permute-done | bytes 393248 | tf_op jit(solution)/shard_map/ppermute | solution.py:238
  44.7 4.0 %collective-permute-done.6 = bf16[4,64,768]{2,1,0:T(8,128)(2,1)S(1)} collective-permute-done((bf16[4,64,768]{2,1,0:T(8,128)(2,1)S(1)}, bf16[4,64,768]{2,1,0:T(8,128)(2,1)S(1)}, u32[]{:S(2)}, u32[]{:S(2)}) %collective-permute-start.6) | collective-permute-done | bytes 393248 | tf_op jit(solution)/shard_map/ppermute | solution.py:38
  48.7 0.9 collective-permute-done.8
  49.6 1.4 %pad_maximum_fusion.own_hbm = bf16[4,4,64,768]{3,2,1,0:T(8,128)(2,1)} fusion(bf16[1,4,64,768]{3,2,1,0:T(8,128)(2,1)S(1)} %bitcast.12, bf16[1,4,64,768]{3,2,1,0:T(8,128)(2,1)S(1)} %bitcast.10, bf16[1,4,64,768]{3,2,1,0:T(8,128)(2,1)S(1)} %bitcast.11, bf16[1,4,64,768]{3,2,1,0:T(8,128)(2,1)S(1)} %bitcast.9), kind=kLoop, calls=%fused_computation | loop fusion | flops 2359296 | bytes 3145728 | tf_op jit(solution)/shard_map/stack | solution.py:245
  51.0 1.9 %collective-permute-start.9 = (bf16[4,4,64,768]{3,2,1,0:T(8,128)(2,1)}, bf16[4,4,64,768]{3,2,1,0:T(8,128)(2,1)S(1)}, u32[]{:S(2)}, u32[]{:S(2)}) collective-permute-start(bf16[4,4,64,768]{3,2,1,0:T(8,128)(2,1)} %pad_maximum_fusion.own_hbm), channel_id=1, source_target_pairs={{0,8},{8,0},{1,9},{9,1},{2,10},{10,2},{3,11},{11,3},{4,12},{12,4},... | collective-permute-start | bytes 4718600 | tf_op jit(solution)/shard_map/ppermute | solution.py:38
  52.9 4.9 %collective-permute-start.1 = (bf16[256,256]{1,0:T(8,128)(2,1)S(1)}, bf16[256,256]{1,0:T(8,128)(2,1)S(1)}, u32[]{:S(2)}, u32[]{:S(2)}) collective-permute-start(bf16[256,256]{1,0:T(8,128)(2,1)S(1)} %get-tuple-element.11.kv0_ref), channel_id=1, source_target_pairs={{0,16},{8,24},{16,32},{24,40},{32,48},{40,56},{48,64},{56,72},{64,... | collective-permute-start | bytes 393224 | tf_op jit(solution)/shard_map/ppermute | solution.py:33
  57.8 2.1 %collective-permute-start = (bf16[256,256]{1,0:T(8,128)(2,1)S(1)}, bf16[256,256]{1,0:T(8,128)(2,1)S(1)}, u32[]{:S(2)}, u32[]{:S(2)}) collective-permute-start(bf16[256,256]{1,0:T(8,128)(2,1)S(1)} %get-tuple-element.11.kv0_ref), channel_id=1, source_target_pairs={{0,8},{8,16},{16,24},{24,32},{32,40},{40,48},{48,56},{56,64},{64,7... | collective-permute-start | bytes 393224 | tf_op jit(solution)/shard_map/ppermute | solution.py:33
  60.0 3.1 %collective-permute-done.1.kv2_ref = bf16[256,256]{1,0:T(8,128)(2,1)S(1)} collective-permute-done((bf16[256,256]{1,0:T(8,128)(2,1)S(1)}, bf16[256,256]{1,0:T(8,128)(2,1)S(1)}, u32[]{:S(2)}, u32[]{:S(2)}) %collective-permute-start.1) | collective-permute-done | bytes 131104 | tf_op jit(solution)/shard_map/ppermute | solution.py:33
  63.1 3.4 %collective-permute-done.kv1_ref = bf16[256,256]{1,0:T(8,128)(2,1)S(1)} collective-permute-done((bf16[256,256]{1,0:T(8,128)(2,1)S(1)}, bf16[256,256]{1,0:T(8,128)(2,1)S(1)}, u32[]{:S(2)}, u32[]{:S(2)}) %collective-permute-start) | collective-permute-done | bytes 131104 | tf_op jit(solution)/shard_map/ppermute | solution.py:33
  66.5 3.7 %attention.1 = (bf16[256,512]{1,0:T(8,128)(2,1)S(1)}, f32[256,256]{1,0:T(8,128)S(1)}, bf16[256,256]{1,0:T(8,128)(2,1)S(1)}, bf16[256,256]{1,0:T(8,128)(2,1)S(1)}) custom-call(s32[3,2,4]{2,1,0:T(2,128)} %bitcast.13, bf16[256,512]{1,0:T(8,128)(2,1)} %q_ref.1, bf16[256,512]{1,0:T(8,128)(2,1)} %do_ref.1, bf16[256,512]{1,0:T(8,128)(2,1)} %o_ref.1, ...), custom_call_target="tpu_custom_call" | custom-call | tf_op jit(solution)/shard_map/attention/pallas_call | solution.py:111
  70.2 1.9 %collective-permute-start.3 = (bf16[256,256]{1,0:T(8,128)(2,1)S(1)}, bf16[256,256]{1,0:T(8,128)(2,1)S(1)}, u32[]{:S(2)}, u32[]{:S(2)}) collective-permute-start(bf16[256,256]{1,0:T(8,128)(2,1)S(1)} %get-tuple-element.14), channel_id=1, source_target_pairs={{8,0},{16,8},{24,16},{32,24},{40,32},{48,40},{56,48},{64,56},{72,6... | collective-permute-start | bytes 393224 | tf_op jit(solution)/shard_map/ppermute | solution.py:33
  72.1 2.8 %collective-permute-start.4 = (bf16[256,256]{1,0:T(8,128)(2,1)S(1)}, bf16[256,256]{1,0:T(8,128)(2,1)S(1)}, u32[]{:S(2)}, u32[]{:S(2)}) collective-permute-start(bf16[256,256]{1,0:T(8,128)(2,1)S(1)} %get-tuple-element.15), channel_id=1, source_target_pairs={{16,0},{24,8},{32,16},{40,24},{48,32},{56,40},{64,48},{72,56},{80,... | collective-permute-start | bytes 393224 | tf_op jit(solution)/shard_map/ppermute | solution.py:33
  74.9 4.6 %collective-permute-start.2 = (bf16[256,512]{1,0:T(8,128)(2,1)S(1)}, bf16[256,512]{1,0:T(8,128)(2,1)S(1)}, u32[]{:S(2)}, u32[]{:S(2)}) collective-permute-start(bf16[256,512]{1,0:T(8,128)(2,1)S(1)} %get-tuple-element.12.q_ref), channel_id=1, source_target_pairs={{0,16},{16,0},{1,17},{17,1},{2,18},{18,2},{3,19},{19,3},{4,20},{20... | collective-permute-start | bytes 786440 | tf_op jit(solution)/shard_map/ppermute | solution.py:38
  79.5 0.0 collective-permute-done.3
  79.5 2.2 %collective-permute-done.4 = bf16[256,256]{1,0:T(8,128)(2,1)S(1)} collective-permute-done((bf16[256,256]{1,0:T(8,128)(2,1)S(1)}, bf16[256,256]{1,0:T(8,128)(2,1)S(1)}, u32[]{:S(2)}, u32[]{:S(2)}) %collective-permute-start.4) | collective-permute-done | bytes 131104 | tf_op jit(solution)/shard_map/ppermute | solution.py:33
  81.7 0.1 add_convert_fusion.kv_ref
  81.8 2.6 %collective-permute-start.5 = (bf16[256,256]{1,0:T(8,128)(2,1)S(1)}, bf16[256,256]{1,0:T(8,128)(2,1)S(1)}, u32[]{:S(2)}, u32[]{:S(2)}) collective-permute-start(bf16[256,256]{1,0:T(8,128)(2,1)S(1)} %add_convert_fusion.kv_ref), channel_id=1, source_target_pairs={{0,16},{16,0},{1,17},{17,1},{2,18},{18,2},{3,19},{19,3},{4,20},{20... | collective-permute-start | bytes 393224 | tf_op jit(solution)/shard_map/ppermute | solution.py:38
  84.4 0.0 collective-permute-done.9.other_ref
  84.4 3.4 %shard_map.100.rest_0_ = bf16[16,256,256]{2,1,0:T(8,128)(2,1)} custom-call(bf16[256,512]{1,0:T(8,128)(2,1)S(1)} %get-tuple-element.12.q_ref, bf16[256,256]{1,0:T(8,128)(2,1)S(1)} %add_convert_fusion.kv_ref, bf16[4,4,64,768]{3,2,1,0:T(8,128)(2,1)} %pad_maximum_fusion.own_hbm, bf16[4,4,64,768]{3,2,1,0:T(8,128)(2,1)S(1)} %collective-permute-done.9.other_ref), custom_call_target="tpu_custom_call" | custom-call | tf_op jit(solution)/shard_map/pallas_call | solution.py:167
  87.9 2.3 %collective-permute-done.5.kv_ref = bf16[256,256]{1,0:T(8,128)(2,1)S(1)} collective-permute-done((bf16[256,256]{1,0:T(8,128)(2,1)S(1)}, bf16[256,256]{1,0:T(8,128)(2,1)S(1)}, u32[]{:S(2)}, u32[]{:S(2)}) %collective-permute-start.5) | collective-permute-done | bytes 131104 | tf_op jit(solution)/shard_map/ppermute | solution.py:38
  90.2 0.0 collective-permute-done.2.q_ref
  90.2 3.5 %shard_map.101 = bf16[16,256,256]{2,1,0:T(8,128)(2,1)} custom-call(bf16[256,512]{1,0:T(8,128)(2,1)S(1)} %collective-permute-done.2.q_ref, bf16[256,256]{1,0:T(8,128)(2,1)S(1)} %collective-permute-done.5.kv_ref, bf16[4,4,64,768]{3,2,1,0:T(8,128)(2,1)} %pad_maximum_fusion.own_hbm, ...), custom_call_target="tpu_custom_call", output_to_operand_aliasing={{}: (4, {})} | custom-call | tf_op jit(solution)/shard_map/pallas_call | solution.py:167
  93.6 33.9 %all_to_all.5.in_ref = bf16[16,256,256]{2,1,0:T(8,128)(2,1)S(1)} all-to-all(bf16[16,256,256]{2,1,0:T(8,128)(2,1)} %shard_map.101), channel_id=1, replica_groups=mesh['zh'=4,'zl'=4,'xh'=2,'core'=2,'xl'=2,'y'=4] {'xh','xl','y'}, dimensions={0} | all-to-all | bytes 4194304 | tf_op jit(solution)/shard_map/all_to_all | solution.py:251
  127.6 1.0 total.1
Async XLA Ops:
  30.2 14.5 %collective-permute-start.7 = (bf16[4,64,768]{2,1,0:T(8,128)(2,1)S(1)}, bf16[4,64,768]{2,1,0:T(8,128)(2,1)S(1)}, u32[]{:S(2)}, u32[]{:S(2)}) collective-permute-start(bf16[4,64,768]{2,1,0:T(8,128)(2,1)S(1)} %bitcast.6), channel_id=1, source_target_pairs={{64,0},{480,32},{128,64},{32,96},{192,128},{96,160},{256,192},{160... | collective-permute-start | bytes 1179656 | tf_op jit(solution)/shard_map/ppermute | solution.py:238
  33.7 14.9 %collective-permute-start.6 = (bf16[4,64,768]{2,1,0:T(8,128)(2,1)S(1)}, bf16[4,64,768]{2,1,0:T(8,128)(2,1)S(1)}, u32[]{:S(2)}, u32[]{:S(2)}) collective-permute-start(bf16[4,64,768]{2,1,0:T(8,128)(2,1)S(1)} %bitcast.7), channel_id=1, source_target_pairs={{0,480},{32,0},{64,32},{96,64},{128,96},{160,128},{192,160},{224,1... | collective-permute-start | bytes 1179656 | tf_op jit(solution)/shard_map/ppermute | solution.py:38
  36.9 12.8 %collective-permute-start.8 = (bf16[4,64,768]{2,1,0:T(8,128)(2,1)S(1)}, bf16[4,64,768]{2,1,0:T(8,128)(2,1)S(1)}, u32[]{:S(2)}, u32[]{:S(2)}) collective-permute-start(bf16[4,64,768]{2,1,0:T(8,128)(2,1)S(1)} %bitcast.8), channel_id=1, source_target_pairs={{0,32},{32,64},{64,96},{96,128},{128,160},{160,192},{192,224},{224... | collective-permute-start | bytes 1179656 | tf_op jit(solution)/shard_map/ppermute | solution.py:38
  51.0 33.4 %collective-permute-start.9 = (bf16[4,4,64,768]{3,2,1,0:T(8,128)(2,1)}, bf16[4,4,64,768]{3,2,1,0:T(8,128)(2,1)S(1)}, u32[]{:S(2)}, u32[]{:S(2)}) collective-permute-start(bf16[4,4,64,768]{3,2,1,0:T(8,128)(2,1)} %pad_maximum_fusion.own_hbm), channel_id=1, source_target_pairs={{0,8},{8,0},{1,9},{9,1},{2,10},{10,2},{3,11},{11,3},{4,12},{12,4},... | collective-permute-start | bytes 4718600 | tf_op jit(solution)/shard_map/ppermute | solution.py:38
  52.9 10.2 %collective-permute-start.1 = (bf16[256,256]{1,0:T(8,128)(2,1)S(1)}, bf16[256,256]{1,0:T(8,128)(2,1)S(1)}, u32[]{:S(2)}, u32[]{:S(2)}) collective-permute-start(bf16[256,256]{1,0:T(8,128)(2,1)S(1)} %get-tuple-element.11.kv0_ref), channel_id=1, source_target_pairs={{0,16},{8,24},{16,32},{24,40},{32,48},{40,56},{48,64},{56,72},{64,... | collective-permute-start | bytes 393224 | tf_op jit(solution)/shard_map/ppermute | solution.py:33
  57.8 8.7 %collective-permute-start = (bf16[256,256]{1,0:T(8,128)(2,1)S(1)}, bf16[256,256]{1,0:T(8,128)(2,1)S(1)}, u32[]{:S(2)}, u32[]{:S(2)}) collective-permute-start(bf16[256,256]{1,0:T(8,128)(2,1)S(1)} %get-tuple-element.11.kv0_ref), channel_id=1, source_target_pairs={{0,8},{8,16},{16,24},{24,32},{32,40},{40,48},{48,56},{56,64},{64,7... | collective-permute-start | bytes 393224 | tf_op jit(solution)/shard_map/ppermute | solution.py:33
  70.2 9.3 %collective-permute-start.3 = (bf16[256,256]{1,0:T(8,128)(2,1)S(1)}, bf16[256,256]{1,0:T(8,128)(2,1)S(1)}, u32[]{:S(2)}, u32[]{:S(2)}) collective-permute-start(bf16[256,256]{1,0:T(8,128)(2,1)S(1)} %get-tuple-element.14), channel_id=1, source_target_pairs={{8,0},{16,8},{24,16},{32,24},{40,32},{48,40},{56,48},{64,56},{72,6... | collective-permute-start | bytes 393224 | tf_op jit(solution)/shard_map/ppermute | solution.py:33
  72.1 9.6 %collective-permute-start.4 = (bf16[256,256]{1,0:T(8,128)(2,1)S(1)}, bf16[256,256]{1,0:T(8,128)(2,1)S(1)}, u32[]{:S(2)}, u32[]{:S(2)}) collective-permute-start(bf16[256,256]{1,0:T(8,128)(2,1)S(1)} %get-tuple-element.15), channel_id=1, source_target_pairs={{16,0},{24,8},{32,16},{40,24},{48,32},{56,40},{64,48},{72,56},{80,... | collective-permute-start | bytes 393224 | tf_op jit(solution)/shard_map/ppermute | solution.py:33
  74.9 15.2 %collective-permute-start.2 = (bf16[256,512]{1,0:T(8,128)(2,1)S(1)}, bf16[256,512]{1,0:T(8,128)(2,1)S(1)}, u32[]{:S(2)}, u32[]{:S(2)}) collective-permute-start(bf16[256,512]{1,0:T(8,128)(2,1)S(1)} %get-tuple-element.12.q_ref), channel_id=1, source_target_pairs={{0,16},{16,0},{1,17},{17,1},{2,18},{18,2},{3,19},{19,3},{4,20},{20... | collective-permute-start | bytes 786440 | tf_op jit(solution)/shard_map/ppermute | solution.py:38
  81.8 8.4 %collective-permute-start.5 = (bf16[256,256]{1,0:T(8,128)(2,1)S(1)}, bf16[256,256]{1,0:T(8,128)(2,1)S(1)}, u32[]{:S(2)}, u32[]{:S(2)}) collective-permute-start(bf16[256,256]{1,0:T(8,128)(2,1)S(1)} %add_convert_fusion.kv_ref), channel_id=1, source_target_pairs={{0,16},{16,0},{1,17},{17,1},{2,18},{18,2},{3,19},{19,3},{4,20},{20... | collective-permute-start | bytes 393224 | tf_op jit(solution)/shard_map/ppermute | solution.py:38

commit v4 on v3

--- a/solution.py
+++ b/solution.py
@@ -130,21 +130,25 @@
     zl = lax.axis_index("zl")
     xh = lax.axis_index("xh")
     first = 8 * (xh if side == 0 else 1 - xh)
-    loads = [
-        pltpu.make_async_copy(own_hbm.at[:, zh], w_ref.at[:, zh], w_sem.at[zh]) for zh in range(4)
-    ]
-    for load in loads:
-        load.start()
+    loads = []
+    for head in range(8):
+        for e in range(2):
+            k = lax.rem(2 * (head % 2) + e + 4 - zl, 4)
+            loads.append(
+                pltpu.make_async_copy(
+                    own_hbm.at[k, head // 2], w_ref.at[head, e], w_sem.at[head, e]
+                )
+            )
+            loads[-1].start()
     a = jnp.concatenate([q_ref[...], kv_ref[...]], axis=1)
     stores = []
     for head in range(8):
         zh = head // 2
-        if head % 2 == 0:
-            loads[zh].wait()
         wide = []
         for e in range(2):
             k = lax.rem(2 * (head % 2) + e + 4 - zl, 4)
-            wide += [w_ref[k, zh], other_ref[k, zh]]
+            loads[2 * head + e].wait()
+            wide += [w_ref[head, e], other_ref[k, zh]]
         w = jnp.concatenate(wide, axis=0)
         out_ref[head] = dot(a, w, NT).astype(BF)
         stores.append(
@@ -162,7 +166,7 @@
 def project(side, aq, akv, wc, wo, parts=None):
     hbm = pl.BlockSpec(memory_space=pltpu.HBM)
     vm = pl.BlockSpec(memory_space=pltpu.VMEM)
-    rows, _ = wc.shape[2:]
+    rows, cols = wc.shape[2:]
     extra = () if parts is None else (parts,)
     return pl.pallas_call(
         functools.partial(project_kernel, side),
@@ -170,9 +174,9 @@
         in_specs=[vm, vm, hbm, vm] + [hbm] * len(extra),
         out_specs=hbm,
         scratch_shapes=[
-            pltpu.VMEM(wc.shape, BF),
+            pltpu.VMEM((8, 2, rows, cols), BF),
             pltpu.VMEM((8, 256, 4 * rows), BF),
-            pltpu.SemaphoreType.DMA((4,)),
+            pltpu.SemaphoreType.DMA((8, 2)),
             pltpu.SemaphoreType.DMA((8,)),
         ],
         input_output_aliases={4: 0} if extra else {},

time: 129 us -> 131 us (1.016)
  Pallas kernels: 12.6 us -> 15.6 us
  waiting for transfers between devices: 21.1 us -> 19.6 us
    pallas_call x2, Pallas kernels: 6.9 us -> 9.93 us  [project(): pl.pallas_call(functools.partial(project_kernel, side), out_shape=jax.Sha...]
    ppermute x5, waiting for transfers between devices: 7.25 us -> 5.73 us  [shifted(): return lax.ppermute(x, axis, [(i, (i + by) % n) for i in range(n)])]
  transfers between devices with their start and end apart: 10 -> 10, of which waited for: 7 -> 7; matrix products, arithmetic and copies ran while one was open for 0% -> 0% of each run, Pallas kernels for 6% -> 7%
where the time goes in v4:
time: 131 us; the launch traced here: 130 us
  blocking collectives  63.2 us (48%)
  starting transfers between devices  30.2 us (23%)
  waiting for transfers between devices  19.6 us (15%)
  Pallas kernels  15.6 us (12%)
  other arithmetic  1.41 us (1%)
    all_to_all x1, blocking collectives, per_device(): parts = lax.all_to_all(parts, ('xh', 'xl', 'y'), 0, 0)  33.9 us
    all_gather x1, blocking collectives, per_device(): w0 = lax.all_gather(weight, 'zh')  29.2 us
    ppermute x5, starting transfers between devices, shifted(): return lax.ppermute(x, axis, [(i, (i + by) % n) for i in range(n)])  14.9 us
    ppermute x4, starting transfers between devices, passed_along(): return lax.ppermute(x, axis, pairs)  11.8 us
    pallas_call x2, Pallas kernels, project(): pl.pallas_call(functools.partial(project_kernel, side), out_shape=jax.Sha...  9.93 us
    ppermute x4, waiting for transfers between devices, passed_along(): return lax.ppermute(x, axis, pairs)  8.78 us
    ppermute x5, waiting for transfers between devices, shifted(): return lax.ppermute(x, axis, [(i, (i + by) % n) for i in range(n)])  5.73 us
    ppermute x1, waiting for transfers between devices, per_device(): lax.ppermute(w0, Z, [((z + 2 if z % 2 == 0 else z - 2) % 16, z) for z in...  5.05 us
  transfers between devices with their start and end apart: 10, of which 7 were waited for; matrix products, arithmetic and copies ran while one was open for 0% of the time, Pallas kernels for 7%

profile of v4, /device:TPU:32, one launch (start us, length us, event | category | flops | bytes accessed | tf_op | source)
XLA Modules:
  0.0 130.1 jit_solution(4399596117414561616)
XLA Ops:
  0.0 1.0 prepare.1
  1.0 29.2 %all-gather = bf16[256,768]{1,0:T(8,128)(2,1)S(1)} all-gather(bf16[64,768]{1,0:T(8,128)(2,1)S(1)} %get-tuple-element.16), channel_id=2, replica_groups=mesh['zh'=4,'zl'=4,'xh'=2,'core'=2,'xl'=2,'y'=4] {'zh'}, dimensions={0}, use_global_device_ids=true | all-gather | bytes 491520 | tf_op jit(solution)/shard_map/all_gather | solution.py:239
  30.2 3.5 %collective-permute-start.7 = (bf16[4,64,768]{2,1,0:T(8,128)(2,1)S(1)}, bf16[4,64,768]{2,1,0:T(8,128)(2,1)S(1)}, u32[]{:S(2)}, u32[]{:S(2)}) collective-permute-start(bf16[4,64,768]{2,1,0:T(8,128)(2,1)S(1)} %bitcast.6), channel_id=1, source_target_pairs={{64,0},{480,32},{128,64},{32,96},{192,128},{96,160},{256,192},{160... | collective-permute-start | bytes 1179656 | tf_op jit(solution)/shard_map/ppermute | solution.py:242
  33.7 3.1 %collective-permute-start.6 = (bf16[4,64,768]{2,1,0:T(8,128)(2,1)S(1)}, bf16[4,64,768]{2,1,0:T(8,128)(2,1)S(1)}, u32[]{:S(2)}, u32[]{:S(2)}) collective-permute-start(bf16[4,64,768]{2,1,0:T(8,128)(2,1)S(1)} %bitcast.7), channel_id=1, source_target_pairs={{0,480},{32,0},{64,32},{96,64},{128,96},{160,128},{192,160},{224,1... | collective-permute-start | bytes 1179656 | tf_op jit(solution)/shard_map/ppermute | solution.py:38
  36.9 2.7 %collective-permute-start.8 = (bf16[4,64,768]{2,1,0:T(8,128)(2,1)S(1)}, bf16[4,64,768]{2,1,0:T(8,128)(2,1)S(1)}, u32[]{:S(2)}, u32[]{:S(2)}) collective-permute-start(bf16[4,64,768]{2,1,0:T(8,128)(2,1)S(1)} %bitcast.8), channel_id=1, source_target_pairs={{0,32},{32,64},{64,96},{96,128},{128,160},{160,192},{192,224},{224... | collective-permute-start | bytes 1179656 | tf_op jit(solution)/shard_map/ppermute | solution.py:38
  39.6 5.0 %collective-permute-done.7 = bf16[4,64,768]{2,1,0:T(8,128)(2,1)S(1)} collective-permute-done((bf16[4,64,768]{2,1,0:T(8,128)(2,1)S(1)}, bf16[4,64,768]{2,1,0:T(8,128)(2,1)S(1)}, u32[]{:S(2)}, u32[]{:S(2)}) %collective-permute-start.7) | collective-permute-done | bytes 393248 | tf_op jit(solution)/shard_map/ppermute | solution.py:242
  44.7 4.0 %collective-permute-done.6 = bf16[4,64,768]{2,1,0:T(8,128)(2,1)S(1)} collective-permute-done((bf16[4,64,768]{2,1,0:T(8,128)(2,1)S(1)}, bf16[4,64,768]{2,1,0:T(8,128)(2,1)S(1)}, u32[]{:S(2)}, u32[]{:S(2)}) %collective-permute-start.6) | collective-permute-done | bytes 393248 | tf_op jit(solution)/shard_map/ppermute | solution.py:38
  48.7 0.9 collective-permute-done.8
  49.6 1.4 %pad_maximum_fusion.own_hbm = bf16[4,4,64,768]{3,2,1,0:T(8,128)(2,1)} fusion(bf16[1,4,64,768]{3,2,1,0:T(8,128)(2,1)S(1)} %bitcast.12, bf16[1,4,64,768]{3,2,1,0:T(8,128)(2,1)S(1)} %bitcast.10, bf16[1,4,64,768]{3,2,1,0:T(8,128)(2,1)S(1)} %bitcast.11, bf16[1,4,64,768]{3,2,1,0:T(8,128)(2,1)S(1)} %bitcast.9), kind=kLoop, calls=%fused_computation | loop fusion | flops 2359296 | bytes 3145728 | tf_op jit(solution)/shard_map/stack | solution.py:249
  51.0 1.9 %collective-permute-start.9 = (bf16[4,4,64,768]{3,2,1,0:T(8,128)(2,1)}, bf16[4,4,64,768]{3,2,1,0:T(8,128)(2,1)S(1)}, u32[]{:S(2)}, u32[]{:S(2)}) collective-permute-start(bf16[4,4,64,768]{3,2,1,0:T(8,128)(2,1)} %pad_maximum_fusion.own_hbm), channel_id=1, source_target_pairs={{0,8},{8,0},{1,9},{9,1},{2,10},{10,2},{3,11},{11,3},{4,12},{12,4},... | collective-permute-start | bytes 4718600 | tf_op jit(solution)/shard_map/ppermute | solution.py:38
  52.9 4.9 %collective-permute-start.1 = (bf16[256,256]{1,0:T(8,128)(2,1)S(1)}, bf16[256,256]{1,0:T(8,128)(2,1)S(1)}, u32[]{:S(2)}, u32[]{:S(2)}) collective-permute-start(bf16[256,256]{1,0:T(8,128)(2,1)S(1)} %get-tuple-element.11.kv0_ref), channel_id=1, source_target_pairs={{0,16},{8,24},{16,32},{24,40},{32,48},{40,56},{48,64},{56,72},{64,... | collective-permute-start | bytes 393224 | tf_op jit(solution)/shard_map/ppermute | solution.py:33
  57.8 2.1 %collective-permute-start = (bf16[256,256]{1,0:T(8,128)(2,1)S(1)}, bf16[256,256]{1,0:T(8,128)(2,1)S(1)}, u32[]{:S(2)}, u32[]{:S(2)}) collective-permute-start(bf16[256,256]{1,0:T(8,128)(2,1)S(1)} %get-tuple-element.11.kv0_ref), channel_id=1, source_target_pairs={{0,8},{8,16},{16,24},{24,32},{32,40},{40,48},{48,56},{56,64},{64,7... | collective-permute-start | bytes 393224 | tf_op jit(solution)/shard_map/ppermute | solution.py:33
  60.0 3.1 %collective-permute-done.1.kv2_ref = bf16[256,256]{1,0:T(8,128)(2,1)S(1)} collective-permute-done((bf16[256,256]{1,0:T(8,128)(2,1)S(1)}, bf16[256,256]{1,0:T(8,128)(2,1)S(1)}, u32[]{:S(2)}, u32[]{:S(2)}) %collective-permute-start.1) | collective-permute-done | bytes 131104 | tf_op jit(solution)/shard_map/ppermute | solution.py:33
  63.1 3.4 %collective-permute-done.kv1_ref = bf16[256,256]{1,0:T(8,128)(2,1)S(1)} collective-permute-done((bf16[256,256]{1,0:T(8,128)(2,1)S(1)}, bf16[256,256]{1,0:T(8,128)(2,1)S(1)}, u32[]{:S(2)}, u32[]{:S(2)}) %collective-permute-start) | collective-permute-done | bytes 131104 | tf_op jit(solution)/shard_map/ppermute | solution.py:33
  66.5 3.7 %attention.1 = (bf16[256,512]{1,0:T(8,128)(2,1)S(1)}, f32[256,256]{1,0:T(8,128)S(1)}, bf16[256,256]{1,0:T(8,128)(2,1)S(1)}, bf16[256,256]{1,0:T(8,128)(2,1)S(1)}) custom-call(s32[3,2,4]{2,1,0:T(2,128)} %bitcast.13, bf16[256,512]{1,0:T(8,128)(2,1)} %q_ref.1, bf16[256,512]{1,0:T(8,128)(2,1)} %do_ref.1, bf16[256,512]{1,0:T(8,128)(2,1)} %o_ref.1, ...), custom_call_target="tpu_custom_call" | custom-call | tf_op jit(solution)/shard_map/attention/pallas_call | solution.py:111
  70.2 1.9 %collective-permute-start.3 = (bf16[256,256]{1,0:T(8,128)(2,1)S(1)}, bf16[256,256]{1,0:T(8,128)(2,1)S(1)}, u32[]{:S(2)}, u32[]{:S(2)}) collective-permute-start(bf16[256,256]{1,0:T(8,128)(2,1)S(1)} %get-tuple-element.14), channel_id=1, source_target_pairs={{8,0},{16,8},{24,16},{32,24},{40,32},{48,40},{56,48},{64,56},{72,6... | collective-permute-start | bytes 393224 | tf_op jit(solution)/shard_map/ppermute | solution.py:33
  72.1 2.8 %collective-permute-start.4 = (bf16[256,256]{1,0:T(8,128)(2,1)S(1)}, bf16[256,256]{1,0:T(8,128)(2,1)S(1)}, u32[]{:S(2)}, u32[]{:S(2)}) collective-permute-start(bf16[256,256]{1,0:T(8,128)(2,1)S(1)} %get-tuple-element.15), channel_id=1, source_target_pairs={{16,0},{24,8},{32,16},{40,24},{48,32},{56,40},{64,48},{72,56},{80,... | collective-permute-start | bytes 393224 | tf_op jit(solution)/shard_map/ppermute | solution.py:33
  74.9 4.6 %collective-permute-start.2 = (bf16[256,512]{1,0:T(8,128)(2,1)S(1)}, bf16[256,512]{1,0:T(8,128)(2,1)S(1)}, u32[]{:S(2)}, u32[]{:S(2)}) collective-permute-start(bf16[256,512]{1,0:T(8,128)(2,1)S(1)} %get-tuple-element.12.q_ref), channel_id=1, source_target_pairs={{0,16},{16,0},{1,17},{17,1},{2,18},{18,2},{3,19},{19,3},{4,20},{20... | collective-permute-start | bytes 786440 | tf_op jit(solution)/shard_map/ppermute | solution.py:38
  79.5 0.0 collective-permute-done.3
  79.5 2.2 %collective-permute-done.4 = bf16[256,256]{1,0:T(8,128)(2,1)S(1)} collective-permute-done((bf16[256,256]{1,0:T(8,128)(2,1)S(1)}, bf16[256,256]{1,0:T(8,128)(2,1)S(1)}, u32[]{:S(2)}, u32[]{:S(2)}) %collective-permute-start.4) | collective-permute-done | bytes 131104 | tf_op jit(solution)/shard_map/ppermute | solution.py:33
  81.7 0.1 add_convert_fusion.kv_ref
  81.8 2.6 %collective-permute-start.5 = (bf16[256,256]{1,0:T(8,128)(2,1)S(1)}, bf16[256,256]{1,0:T(8,128)(2,1)S(1)}, u32[]{:S(2)}, u32[]{:S(2)}) collective-permute-start(bf16[256,256]{1,0:T(8,128)(2,1)S(1)} %add_convert_fusion.kv_ref), channel_id=1, source_target_pairs={{0,16},{16,0},{1,17},{17,1},{2,18},{18,2},{3,19},{19,3},{4,20},{20... | collective-permute-start | bytes 393224 | tf_op jit(solution)/shard_map/ppermute | solution.py:38
  84.4 0.0 collective-permute-done.9.other_ref
  84.4 5.0 %shard_map.100.rest_0_ = bf16[16,256,256]{2,1,0:T(8,128)(2,1)} custom-call(bf16[256,512]{1,0:T(8,128)(2,1)S(1)} %get-tuple-element.12.q_ref, bf16[256,256]{1,0:T(8,128)(2,1)S(1)} %add_convert_fusion.kv_ref, bf16[4,4,64,768]{3,2,1,0:T(8,128)(2,1)} %pad_maximum_fusion.own_hbm, bf16[4,4,64,768]{3,2,1,0:T(8,128)(2,1)S(1)} %collective-permute-done.9.other_ref), custom_call_target="tpu_custom_call" | custom-call | tf_op jit(solution)/shard_map/pallas_call | solution.py:171
  89.4 0.8 collective-permute-done.5.kv_ref
  90.2 0.0 collective-permute-done.2.q_ref
  90.2 5.0 %shard_map.101 = bf16[16,256,256]{2,1,0:T(8,128)(2,1)} custom-call(bf16[256,512]{1,0:T(8,128)(2,1)S(1)} %collective-permute-done.2.q_ref, bf16[256,256]{1,0:T(8,128)(2,1)S(1)} %collective-permute-done.5.kv_ref, bf16[4,4,64,768]{3,2,1,0:T(8,128)(2,1)} %pad_maximum_fusion.own_hbm, ...), custom_call_target="tpu_custom_call", output_to_operand_aliasing={{}: (4, {})} | custom-call | tf_op jit(solution)/shard_map/pallas_call | solution.py:171
  95.1 33.9 %all_to_all.5.in_ref = bf16[16,256,256]{2,1,0:T(8,128)(2,1)S(1)} all-to-all(bf16[16,256,256]{2,1,0:T(8,128)(2,1)} %shard_map.101), channel_id=1, replica_groups=mesh['zh'=4,'zl'=4,'xh'=2,'core'=2,'xl'=2,'y'=4] {'xh','xl','y'}, dimensions={0} | all-to-all | bytes 4194304 | tf_op jit(solution)/shard_map/all_to_all | solution.py:255
  129.1 1.0 total.1
Async XLA Ops:
  30.2 14.5 %collective-permute-start.7 = (bf16[4,64,768]{2,1,0:T(8,128)(2,1)S(1)}, bf16[4,64,768]{2,1,0:T(8,128)(2,1)S(1)}, u32[]{:S(2)}, u32[]{:S(2)}) collective-permute-start(bf16[4,64,768]{2,1,0:T(8,128)(2,1)S(1)} %bitcast.6), channel_id=1, source_target_pairs={{64,0},{480,32},{128,64},{32,96},{192,128},{96,160},{256,192},{160... | collective-permute-start | bytes 1179656 | tf_op jit(solution)/shard_map/ppermute | solution.py:242
  33.7 14.9 %collective-permute-start.6 = (bf16[4,64,768]{2,1,0:T(8,128)(2,1)S(1)}, bf16[4,64,768]{2,1,0:T(8,128)(2,1)S(1)}, u32[]{:S(2)}, u32[]{:S(2)}) collective-permute-start(bf16[4,64,768]{2,1,0:T(8,128)(2,1)S(1)} %bitcast.7), channel_id=1, source_target_pairs={{0,480},{32,0},{64,32},{96,64},{128,96},{160,128},{192,160},{224,1... | collective-permute-start | bytes 1179656 | tf_op jit(solution)/shard_map/ppermute | solution.py:38
  36.9 12.8 %collective-permute-start.8 = (bf16[4,64,768]{2,1,0:T(8,128)(2,1)S(1)}, bf16[4,64,768]{2,1,0:T(8,128)(2,1)S(1)}, u32[]{:S(2)}, u32[]{:S(2)}) collective-permute-start(bf16[4,64,768]{2,1,0:T(8,128)(2,1)S(1)} %bitcast.8), channel_id=1, source_target_pairs={{0,32},{32,64},{64,96},{96,128},{128,160},{160,192},{192,224},{224... | collective-permute-start | bytes 1179656 | tf_op jit(solution)/shard_map/ppermute | solution.py:38
  51.0 33.4 %collective-permute-start.9 = (bf16[4,4,64,768]{3,2,1,0:T(8,128)(2,1)}, bf16[4,4,64,768]{3,2,1,0:T(8,128)(2,1)S(1)}, u32[]{:S(2)}, u32[]{:S(2)}) collective-permute-start(bf16[4,4,64,768]{3,2,1,0:T(8,128)(2,1)} %pad_maximum_fusion.own_hbm), channel_id=1, source_target_pairs={{0,8},{8,0},{1,9},{9,1},{2,10},{10,2},{3,11},{11,3},{4,12},{12,4},... | collective-permute-start | bytes 4718600 | tf_op jit(solution)/shard_map/ppermute | solution.py:38
  52.9 10.2 %collective-permute-start.1 = (bf16[256,256]{1,0:T(8,128)(2,1)S(1)}, bf16[256,256]{1,0:T(8,128)(2,1)S(1)}, u32[]{:S(2)}, u32[]{:S(2)}) collective-permute-start(bf16[256,256]{1,0:T(8,128)(2,1)S(1)} %get-tuple-element.11.kv0_ref), channel_id=1, source_target_pairs={{0,16},{8,24},{16,32},{24,40},{32,48},{40,56},{48,64},{56,72},{64,... | collective-permute-start | bytes 393224 | tf_op jit(solution)/shard_map/ppermute | solution.py:33
  57.8 8.7 %collective-permute-start = (bf16[256,256]{1,0:T(8,128)(2,1)S(1)}, bf16[256,256]{1,0:T(8,128)(2,1)S(1)}, u32[]{:S(2)}, u32[]{:S(2)}) collective-permute-start(bf16[256,256]{1,0:T(8,128)(2,1)S(1)} %get-tuple-element.11.kv0_ref), channel_id=1, source_target_pairs={{0,8},{8,16},{16,24},{24,32},{32,40},{40,48},{48,56},{56,64},{64,7... | collective-permute-start | bytes 393224 | tf_op jit(solution)/shard_map/ppermute | solution.py:33
  70.2 9.3 %collective-permute-start.3 = (bf16[256,256]{1,0:T(8,128)(2,1)S(1)}, bf16[256,256]{1,0:T(8,128)(2,1)S(1)}, u32[]{:S(2)}, u32[]{:S(2)}) collective-permute-start(bf16[256,256]{1,0:T(8,128)(2,1)S(1)} %get-tuple-element.14), channel_id=1, source_target_pairs={{8,0},{16,8},{24,16},{32,24},{40,32},{48,40},{56,48},{64,56},{72,6... | collective-permute-start | bytes 393224 | tf_op jit(solution)/shard_map/ppermute | solution.py:33
  72.1 9.6 %collective-permute-start.4 = (bf16[256,256]{1,0:T(8,128)(2,1)S(1)}, bf16[256,256]{1,0:T(8,128)(2,1)S(1)}, u32[]{:S(2)}, u32[]{:S(2)}) collective-permute-start(bf16[256,256]{1,0:T(8,128)(2,1)S(1)} %get-tuple-element.15), channel_id=1, source_target_pairs={{16,0},{24,8},{32,16},{40,24},{48,32},{56,40},{64,48},{72,56},{80,... | collective-permute-start | bytes 393224 | tf_op jit(solution)/shard_map/ppermute | solution.py:33
  74.9 15.2 %collective-permute-start.2 = (bf16[256,512]{1,0:T(8,128)(2,1)S(1)}, bf16[256,512]{1,0:T(8,128)(2,1)S(1)}, u32[]{:S(2)}, u32[]{:S(2)}) collective-permute-start(bf16[256,512]{1,0:T(8,128)(2,1)S(1)} %get-tuple-element.12.q_ref), channel_id=1, source_target_pairs={{0,16},{16,0},{1,17},{17,1},{2,18},{18,2},{3,19},{19,3},{4,20},{20... | collective-permute-start | bytes 786440 | tf_op jit(solution)/shard_map/ppermute | solution.py:38
  81.8 8.4 %collective-permute-start.5 = (bf16[256,256]{1,0:T(8,128)(2,1)S(1)}, bf16[256,256]{1,0:T(8,128)(2,1)S(1)}, u32[]{:S(2)}, u32[]{:S(2)}) collective-permute-start(bf16[256,256]{1,0:T(8,128)(2,1)S(1)} %add_convert_fusion.kv_ref), channel_id=1, source_target_pairs={{0,16},{16,0},{1,17},{17,1},{2,18},{18,2},{3,19},{19,3},{4,20},{20... | collective-permute-start | bytes 393224 | tf_op jit(solution)/shard_map/ppermute | solution.py:38
